TPU v7x, 32 devices: a whole 2x2x4 slice. The times are simulated.
32 devices in a mesh: dp: 8 (over y, x, core), seq: 4 (over z).
Axes of the slice: x: 2, y: 2, z: 4, core: 2. Of those that a mesh axis runs over, the one named last changes fastest.
Arguments:
- block_input: bfloat16 [4096, 1024], P(('dp', 'seq')), may hold values from -6 to 6
- cotangent: bfloat16 [4096, 1024], P(('dp', 'seq')), may hold values from -6 to 6
- ln1_gain: bfloat16 [1024], P(('dp', 'seq')), may hold values from 0.5 to 1.5
- ln1_bias: bfloat16 [1024], P(('dp', 'seq')), may hold values from -3 to 3
- qkv_weight: bfloat16 [1024, 3072], P(('dp', 'seq')), may hold values from -0.25 to 0.25
- qv_bias: bfloat16 [2048], P(('dp', 'seq')), may hold values from -3 to 3
- out_weight: bfloat16 [1024, 1024], P(('dp', 'seq')), may hold values from -0.75 to 0.75
- out_bias: bfloat16 [1024], P(('dp', 'seq')), may hold values from -3 to 3
- ln2_gain: bfloat16 [1024], P(('dp', 'seq')), may hold values from 0.5 to 1.5
- ln2_bias: bfloat16 [1024], P(('dp', 'seq')), may hold values from -3 to 3
- fc_weight: bfloat16 [1024, 4096], P(('dp', 'seq')), may hold values from -0.1875 to 0.1875
- fc_bias: bfloat16 [4096], P(('dp', 'seq')), may hold values from -3 to 3
- proj_weight: bfloat16 [4096, 1024], P(('dp', 'seq')), may hold values from -0.09375 to 0.09375
- proj_bias: bfloat16 [1024], P(('dp', 'seq')), may hold values from -3 to 3
Outputs:
- block_output: float32 [4096, 1024], P(('dp', 'seq'))
- grad_input: float32 [4096, 1024], P(('dp', 'seq'))
- grad_ln1_gain: float32 [1024], P(('dp', 'seq'))
- grad_ln1_bias: float32 [1024], P(('dp', 'seq'))
- grad_qkv_weight: float32 [1024, 3072], P(('dp', 'seq'))
- grad_qv_bias: float32 [2048], P(('dp', 'seq'))
- grad_out_weight: float32 [1024, 1024], P(('dp', 'seq'))
- grad_out_bias: float32 [1024], P(('dp', 'seq'))
- grad_ln2_gain: float32 [1024], P(('dp', 'seq'))
- grad_ln2_bias: float32 [1024], P(('dp', 'seq'))
- grad_fc_weight: float32 [1024, 4096], P(('dp', 'seq'))
- grad_fc_bias: float32 [4096], P(('dp', 'seq'))
- grad_proj_weight: float32 [4096, 1024], P(('dp', 'seq'))
- grad_proj_bias: float32 [1024], P(('dp', 'seq'))
All inputs are finite; a program needn't handle non-finite values.
Results may differ from a plain program's by a relative error of at most 0.02.
Values may be sent and summed in bfloat16 or wider, within the bound.
A program may use at most 192 MiB of HBM per device.

v0:
```python
import math

import jax
import jax.numpy as jnp
from jax import lax
from jax.experimental import pallas as pl
from jax.experimental.pallas import tpu as pltpu
from jax.sharding import PartitionSpec as P

D = 1024
H = 16
HD = 64
FF = 4096


EPS = 1e-05
GELU_COEF = math.sqrt(2.0 / math.pi)
MESH = pl.DeviceIdType.MESH


def layer_norm(values, norm_gain, offset):
    center = jnp.mean(values, axis=-1, keepdims=True)
    centred = values - center
    spread = jnp.mean(centred * centred, axis=-1, keepdims=True)
    return centred * lax.rsqrt(spread + EPS) * norm_gain + offset


def gelu_tanh(pre_act):
    return (
        0.5
        * pre_act
        * (1.0 + jnp.tanh(GELU_COEF * (pre_act + 0.044715 * pre_act * pre_act * pre_act)))
    )


def halved(values):
    return values.astype(jnp.bfloat16)


def widened(values):
    return values.astype(jnp.float32)


def matmul(left, right):
    return jnp.dot(left, right, preferred_element_type=jnp.float32)


def place():
    return lax.axis_index("dp"), lax.axis_index("seq")


def counts():
    return lax.axis_size("dp"), lax.axis_size("seq")


def remote(src, dst, send, recv, device):
    return pltpu.make_async_remote_copy(
        src_ref=src, dst_ref=dst, send_sem=send, recv_sem=recv, device_id=device, device_id_type=MESH
    )


def dma(*shape):
    return pltpu.SemaphoreType.DMA(shape)


def greet_all():
    dp, s = place()
    dpc, n = counts()
    barrier = pltpu.get_barrier_semaphore()

    def greet(i, carry):
        @pl.when(i != dp * n + s)
        def _():
            pl.semaphore_signal(barrier, inc=1, device_id=(i // n, i % n), device_id_type=MESH)

        return carry

    lax.fori_loop(0, dpc * n, greet, 0)
    pl.semaphore_wait(barrier, dpc * n - 1)


def greet_near():
    dp, s = place()
    dpc, n = counts()
    nc = dpc // 2
    barrier = pltpu.get_barrier_semaphore()
    for k in range(1, n):
        pl.semaphore_signal(barrier, inc=1, device_id=(dp, (s + k) % n), device_id_type=MESH)
    for k in range(1, nc):
        pl.semaphore_signal(barrier, inc=1, device_id=((dp + 2 * k) % dpc, s), device_id_type=MESH)
    pl.semaphore_signal(barrier, inc=1, device_id=(other_core(dp), s), device_id_type=MESH)
    pl.semaphore_wait(barrier, n - 1 + nc)


def greet_seq():
    dp, s = place()
    _, n = counts()
    barrier = pltpu.get_barrier_semaphore()
    for k in range(1, n):
        pl.semaphore_signal(barrier, inc=1, device_id=(dp, (s + k) % n), device_id_type=MESH)
    pl.semaphore_wait(barrier, n - 1)


def other_core(dp):
    return dp + 1 - 2 * (dp % 2)


class Exchange:
    def __init__(self, value):
        _, n = counts()
        self.operands = (value,)
        self.outs = (value,)
        self.sems = (dma(n), dma(n))

    def copies(self, ins, outs, sems):
        dp, s = place()
        _, n = counts()
        return [
            remote(
                ins[0].at[(s + k) % n], outs[0].at[s], sems[0].at[k], sems[1].at[k], (dp, (s + k) % n)
            )
            for k in range(n - 1, 0, -1)
        ]

    def start(self, ins, outs, sems):
        for copy in self.copies(ins, outs, sems):
            copy.start()

    def finish(self, ins, outs, sems):
        for copy in self.copies(ins, outs, sems):
            copy.wait()


class Plane(Exchange):
    def __init__(self, value):
        dpc, _ = counts()
        self.operands = (value,)
        self.outs = (value,)
        self.sems = (dma(dpc // 2), dma(dpc // 2))

    def copies(self, ins, outs, sems):
        dp, s = place()
        dpc, _ = counts()
        chip, core, nc = dp // 2, dp % 2, dpc // 2
        return [
            remote(
                ins[0].at[(chip + k) % nc],
                outs[0].at[chip],
                sems[0].at[k],
                sems[1].at[k],
                ((chip + k) % nc * 2 + core, s),
            )
            for k in range(1, nc)
        ]


class Partner(Exchange):
    def __init__(self, value):
        self.operands = (value,)
        self.outs = (jax.ShapeDtypeStruct(value.shape[1:], value.dtype),)
        self.sems = (dma(1), dma(1))

    def copies(self, ins, outs, sems):
        dp, s = place()
        return [
            remote(
                ins[0].at[1 - dp % 2], outs[0], sems[0].at[0], sems[1].at[0], (other_core(dp), s)
            )
        ]


class Everyone:
    def __init__(self, value):
        dpc, n = counts()
        self.operands = (value,)
        self.outs = (value,)
        self.sems = (dma(dpc * n), dma(dpc * n))

    def copy(self, ins, outs, sems, k):
        dp, s = place()
        dpc, n = counts()
        me = dp * n + s
        peer = (me + k) % (dpc * n)
        return remote(
            ins[0].at[peer], outs[0].at[me], sems[0].at[k], sems[1].at[k], (peer // n, peer % n)
        )

    def start(self, ins, outs, sems):
        def step(k, carry):
            self.copy(ins, outs, sems, k).start()
            return carry

        lax.fori_loop(1, self.outs[0].shape[0], step, 0)

    def finish(self, ins, outs, sems):
        def step(k, carry):
            self.copy(ins, outs, sems, k).wait()
            return carry

        lax.fori_loop(1, self.outs[0].shape[0], step, 0)


class Line:
    def __init__(self, value):
        _, n = counts()
        self.operands = (value,)
        self.outs = (jax.ShapeDtypeStruct((n,) + value.shape, value.dtype),)
        self.sems = (dma(2, n), dma(2, n), dma(1))

    def hand_on(self, ins, outs, sems, way, k):
        dp, s = place()
        sign = 1 - 2 * way
        block = outs[0].at[s - sign * k]
        return remote(
            ins[0] if k == 0 else block, block, sems[0].at[way, k], sems[1].at[way, k], (dp, s + sign)
        )

    def guard(self, way, k):
        _, s = place()
        _, n = counts()
        return (s >= k) if way == 0 else (s < n - k)

    def start(self, ins, outs, sems):
        _, s = place()
        _, n = counts()
        pltpu.make_async_copy(ins[0], outs[0].at[s], sems[2].at[0]).start()
        for way in (0, 1):
            follows = (s < n - 1) if way == 0 else (s > 0)

            @pl.when(follows)
            def _():
                self.hand_on(ins, outs, sems, way, 0).start()

    def step(self, ins, outs, sems, k):
        dp, s = place()
        _, n = counts()
        for way in (0, 1):
            sign = 1 - 2 * way
            follows = (s < n - 1) if way == 0 else (s > 0)

            @pl.when(self.guard(way, k))
            def _():
                block = outs[0].at[s - sign * k]
                remote(
                    block, block, sems[0].at[way, k - 1], sems[1].at[way, k - 1], (dp, s - sign)
                ).wait_recv()
                if k < n - 1:

                    @pl.when(follows)
                    def _():
                        self.hand_on(ins, outs, sems, way, k).start()

    def close(self, ins, outs, sems):
        _, s = place()
        _, n = counts()
        for way in (0, 1):
            follows = (s < n - 1) if way == 0 else (s > 0)
            for k in range(n - 1):

                @pl.when(jnp.logical_and(follows, self.guard(way, k)))
                def _():
                    self.hand_on(ins, outs, sems, way, k).wait_send()

        pltpu.make_async_copy(ins[0], outs[0].at[s], sems[2].at[0]).wait()

    def finish(self, ins, outs, sems):
        _, n = counts()
        for k in range(1, n):
            self.step(ins, outs, sems, k)
        self.close(ins, outs, sems)


class Turn:
    def __init__(self, value, outward):
        self.outward = outward
        self.operands = (value,)
        self.outs = (value,)
        self.sems = (dma(1), dma(1), dma(1))

    def target(self):
        dp, s = place()
        dpc, n = counts()
        if self.outward:
            rank = s * dpc + dp
            return rank // n, rank % n
        rank = dp * n + s
        return rank % dpc, rank // dpc

    def away(self):
        dp, s = place()
        to_dp, to_s = self.target()
        return jnp.logical_or(to_dp != dp, to_s != s)

    def copy(self, ins, outs, sems):
        return remote(ins[0], outs[0], sems[0].at[0], sems[1].at[0], self.target())

    def start(self, ins, outs, sems):
        @pl.when(self.away())
        def _():
            self.copy(ins, outs, sems).start()

        @pl.when(jnp.logical_not(self.away()))
        def _():
            pltpu.make_async_copy(ins[0], outs[0], sems[2].at[0]).start()

    def finish(self, ins, outs, sems):
        @pl.when(self.away())
        def _():
            self.copy(ins, outs, sems).wait()

        @pl.when(jnp.logical_not(self.away()))
        def _():
            pltpu.make_async_copy(ins[0], outs[0], sems[2].at[0]).wait()


def run(number, greet, *tasks):
    spans = []
    a = b = c = 0
    for task in tasks:
        spans.append((a, b, c))
        a += len(task.operands)
        b += len(task.outs)
        c += len(task.sems)
    n_in, n_out = a, b

    def kernel(*refs):
        ins, outs, sems = refs[:n_in], refs[n_in : n_in + n_out], refs[n_in + n_out :]
        greet()
        views = [
            (
                ins[i : i + len(t.operands)],
                outs[o : o + len(t.outs)],
                sems[m : m + len(t.sems)],
            )
            for t, (i, o, m) in zip(tasks, spans)
        ]
        for t, view in zip(tasks, views):
            t.start(*view)
        for t, view in zip(tasks, views):
            t.finish(*view)

    return pl.pallas_call(
        kernel,
        out_shape=[jax.ShapeDtypeStruct(o.shape, o.dtype) for t in tasks for o in t.outs],
        in_specs=[pl.BlockSpec(memory_space=pl.ANY)] * n_in,
        out_specs=[pl.BlockSpec(memory_space=pl.ANY)] * n_out,
        scratch_shapes=[s for t in tasks for s in t.sems],
        compiler_params=pltpu.CompilerParams(collective_id=number, has_side_effects=True),
    )(*[v for t in tasks for v in t.operands])


def gather_inputs(block_input, cotangent, pack, out_rows, proj_rows):
    dpc, n = counts()
    nc = dpc // 2
    tokens, grads = Line(block_input), Line(cotangent)

    def kernel(
        x_in, g_in, pack_in, out_in, proj_in, x_all, g_all, pack_all, out_all, proj_all,
        x_send, x_recv, x_own, g_send, g_recv, g_own, turn_send, turn_recv, local,
        z_send, z_recv, c_send, c_recv, p_send, p_recv,
    ):
        dp, s = place()
        chip, core = dp // 2, dp % 2
        greet_all()
        gathered = (proj_all, out_all, pack_all)
        rank = dp * n + s
        to_dp, to_s = rank % dpc, rank // dpc
        home = jnp.logical_and(to_dp == dp, to_s == s)
        turn = remote(
            out_in, out_all.at[to_dp], turn_send.at[0], turn_recv.at[0], (to_dp, to_s)
        )
        keep_out = pltpu.make_async_copy(out_in, out_all.at[dp], local.at[1])
        keep_pack = pltpu.make_async_copy(pack_in.at[s], pack_all.at[dp, s], local.at[2])
        keep_proj = pltpu.make_async_copy(proj_in, proj_all.at[dp], local.at[0])
        keep_pack.start()
        shuffles = [
            remote(
                pack_in.at[(s + k) % n], pack_all.at[dp, s], z_send.at[k], z_recv.at[k],
                (dp, (s + k) % n),
            )
            for k in range(n - 1, 0, -1)
        ]
        for copy in shuffles:
            copy.start()

        @pl.when(home)
        def _():
            keep_out.start()

        @pl.when(jnp.logical_not(home))
        def _():
            turn.start()

        keep_proj.start()

        def to_chips(a, source):
            return [
                remote(
                    source, gathered[a].at[dp], c_send.at[a, k], c_recv.at[a, k],
                    ((chip + k) % nc * 2 + core, s),
                )
                for k in range(1, nc)
            ]

        def to_partner(a, k, source):
            slot = (chip - k + nc) % nc * 2 + core
            return remote(
                source if source is not None else gathered[a].at[slot],
                gathered[a].at[slot], p_send.at[a, k], p_recv.at[a, k], (other_core(dp), s),
            )

        def arrive(a, k):
            block = gathered[a].at[(chip - k + nc) % nc * 2 + core]
            remote(
                block, block, c_send.at[a, k], c_recv.at[a, k], ((chip - k + nc) % nc * 2 + core, s)
            ).wait_recv()

        sources = (proj_in, out_all.at[dp], pack_all.at[dp])
        tokens.start((x_in,), (x_all,), (x_send, x_recv, x_own))
        for copy in to_chips(0, sources[0]):
            copy.start()
        to_partner(0, 0, sources[0]).start()

        @pl.when(home)
        def _():
            keep_out.wait()

        @pl.when(jnp.logical_not(home))
        def _():
            turn.wait()

        keep_pack.wait()
        for copy in shuffles:
            copy.wait()
        for a in (1, 2):
            for copy in to_chips(a, sources[a]):
                copy.start()
            to_partner(a, 0, sources[a]).start()
        for k in range(1, n):
            tokens.step((x_in,), (x_all,), (x_send, x_recv, x_own), k)
            if k == 1:
                grads.start((g_in,), (g_all,), (g_send, g_recv, g_own))
        for a in range(3):
            for k in range(1, nc):
                arrive(a, k)
                to_partner(a, k, None).start()
        for k in range(1, n):
            grads.step((g_in,), (g_all,), (g_send, g_recv, g_own), k)
        tokens.close((x_in,), (x_all,), (x_send, x_recv, x_own))
        grads.close((g_in,), (g_all,), (g_send, g_recv, g_own))
        for a in range(3):
            for copy in to_chips(a, sources[a]):
                copy.wait_send()
            for k in range(nc):
                slot = (chip - k + nc) % nc * 2 + 1 - core
                to_partner(a, k, sources[a] if k == 0 else None).wait_send()
                block = gathered[a].at[slot]
                remote(
                    block, block, p_send.at[a, k], p_recv.at[a, k], (other_core(dp), s)
                ).wait_recv()
        keep_proj.wait()

    def grown(value, *lead):
        return jax.ShapeDtypeStruct(lead + value.shape, value.dtype)

    return pl.pallas_call(
        kernel,
        out_shape=[
            grown(block_input, n), grown(cotangent, n), grown(pack, dpc), grown(out_rows, dpc),
            grown(proj_rows, dpc),
        ],
        in_specs=[pl.BlockSpec(memory_space=pl.ANY)] * 5,
        out_specs=[pl.BlockSpec(memory_space=pl.ANY)] * 5,
        scratch_shapes=[
            *tokens.sems, *grads.sems, dma(1), dma(1), dma(3),
            dma(n), dma(n), dma(3, nc), dma(3, nc), dma(3, nc), dma(3, nc),
        ],
        compiler_params=pltpu.CompilerParams(collective_id=0, has_side_effects=True),
    )(block_input, cotangent, pack, out_rows, proj_rows)


def total(own, received, mine):
    picked = [
        jnp.where(k == mine, widened(own[k]), widened(received[k])) for k in range(own.shape[0])
    ]
    result = picked[0]
    for value in picked[1:]:
        result = result + value
    return result


def fill(own, received, mine):
    slots = lax.broadcasted_iota(jnp.int32, (own.shape[0],) + (1,) * (own.ndim - 1), 0)
    return jnp.where(slots == mine, own, received)


def local(
    block_input,
    cotangent,
    ln1_gain,
    ln1_bias,
    qkv_weight,
    qv_bias,
    out_weight,
    out_bias,
    ln2_gain,
    ln2_bias,
    fc_weight,
    fc_bias,
    proj_weight,
    proj_bias,
):
    dp, s = place()
    dpc, n = counts()
    nc, ranks = dpc // 2, dpc * n
    core, chip = dp % 2, dp // 2
    tok_rows = block_input.shape[0]
    rows = qkv_weight.shape[0]
    units = fc_bias.shape[0]
    heads = H // n
    wide = heads * HD
    length = n * tok_rows
    score_scale = HD ** (-0.5)

    small = jnp.concatenate(
        [ln1_gain, ln1_bias, out_bias, ln2_gain, ln2_bias, proj_bias, qv_bias, fc_bias]
    )
    margin = -(-small.shape[0] // (rows * 128)) * 128
    block = jnp.pad(small, (0, rows * margin - small.shape[0])).reshape(rows, margin)
    pack = jnp.concatenate(
        [
            qkv_weight.reshape(rows, 3, n, wide).transpose(2, 0, 1, 3).reshape(n, rows, 3 * wide),
            fc_weight.reshape(rows, dpc, n, units).transpose(2, 0, 1, 3).reshape(n, rows, dpc * units),
            jnp.broadcast_to(block[None], (n, rows, margin)),
        ],
        axis=2,
    )
    x_all, g_all, pack_all, out_all, proj_all = gather_inputs(
        block_input, cotangent, pack, out_weight, proj_weight
    )
    stream_seq = widened(x_all.reshape(length, D))
    grad_seq = g_all.reshape(length, D)
    pack_rows = pack_all.reshape(D, pack.shape[2])
    qkv_cols = pack_rows[:, : 3 * wide]
    fc_cols = pack_rows[:, 3 * wide : 3 * wide + dpc * units]
    out_rows = out_all.reshape(wide, D)
    proj_rows = proj_all.reshape(dpc * units, D)
    smalls = pack_rows[:, 3 * wide + dpc * units :].reshape(ranks, rows * margin)
    gain_one, bias_one, out_bias_full, gain_two, bias_two, proj_bias_full = (
        widened(smalls[:, i * rows : (i + 1) * rows].reshape(D)) for i in range(6)
    )
    at = 6 * rows
    qv_full = smalls[:, at : at + qv_bias.shape[0]].reshape(2, n, wide)
    qv_own = widened(lax.dynamic_index_in_dim(qv_full, s, 1, keepdims=False))
    at += qv_bias.shape[0]
    fc_bias_cols = widened(
        lax.dynamic_index_in_dim(
            smalls[:, at : at + units].reshape(dpc, n, units), s, 1, keepdims=False
        ).reshape(dpc * units)
    )

    normed_one = halved(layer_norm(stream_seq, gain_one, bias_one))
    projected = matmul(normed_one, qkv_cols)

    def by_head(values):
        return values.reshape(length, heads, HD).transpose(1, 0, 2)

    def by_token(values):
        return values.transpose(1, 0, 2).reshape(length, wide)

    queries = by_head(halved(projected[:, :wide] + qv_own[0]))
    keys = by_head(halved(projected[:, wide : 2 * wide]))
    values = by_head(halved(projected[:, 2 * wide :] + qv_own[1]))
    position = jnp.arange(length, dtype=jnp.int32)
    visible = position[None, :] <= position[:, None]
    scores = (
        jnp.einsum("hqd,hkd->hqk", queries, keys, preferred_element_type=jnp.float32) * score_scale
    )
    log_total = jnp.log(
        jnp.sum(jnp.where(visible, jnp.exp(scores), 0.0), axis=-1, keepdims=True)
    )
    probs = jnp.where(visible, jnp.exp(scores - log_total), 0.0)
    shares = halved(probs)
    attended_heads = halved(
        jnp.einsum("hqk,hkd->hqd", shares, values, preferred_element_type=jnp.float32)
    )
    attended = by_token(attended_heads)
    mixed = halved(matmul(attended, out_rows)).reshape(n, tok_rows, D)
    (mixed_got,) = run(1, greet_seq, Exchange(mixed))
    stream = widened(block_input)
    middle = stream + total(mixed, mixed_got, s) + out_bias_full
    normed_two = halved(layer_norm(middle, gain_two, bias_two))
    (normed_all,) = run(2, greet_seq, Line(normed_two))
    normed_seq = normed_all.reshape(length, D)
    grad_out = widened(cotangent)
    d_proj_bias = jnp.sum(grad_out, axis=0)
    pre_act = matmul(normed_seq, fc_cols) + fc_bias_cols
    hidden = halved(gelu_tanh(pre_act))
    grad_hidden = matmul(grad_seq, proj_rows.T)
    _, gelu_back = jax.vjp(gelu_tanh, pre_act)
    grad_pre = gelu_back(grad_hidden)[0]
    pre_half = halved(grad_pre)
    back_two = halved(matmul(pre_half, fc_cols.T)).reshape(n, tok_rows, D)
    (back_two_got,) = run(3, greet_seq, Exchange(back_two))
    ff_part = halved(matmul(hidden, proj_rows)).reshape(n, tok_rows, D)

    def by_core(values):
        return halved(values).reshape(nc, 2, -1, values.shape[-1]).transpose(1, 0, 2, 3)

    d_proj = by_core(matmul(hidden.T, grad_seq))
    d_fc = by_core(matmul(normed_seq.T, pre_half))
    d_fc_bias = jnp.sum(grad_pre, axis=0).reshape(dpc, 1, units)
    _, norm_back_two = jax.vjp(layer_norm, middle, gain_two, bias_two)
    mid_branch, d_ln2_gain, d_ln2_bias = norm_back_two(total(back_two, back_two_got, s))
    grad_middle = grad_out + mid_branch
    d_out_bias = jnp.sum(grad_middle, axis=0)
    middle_all, d_proj_got, d_fc_got = run(
        4, greet_near, Line(halved(grad_middle)), Partner(d_proj), Partner(d_fc)
    )

    def pair(own, received):
        kept = lax.dynamic_index_in_dim(own, core, 0, keepdims=False)
        return halved(widened(kept) + widened(received))

    d_proj, d_fc = pair(d_proj, d_proj_got), pair(d_fc, d_fc_got)
    middle_half = middle_all.reshape(length, D)
    d_out = by_core(matmul(attended.T, middle_half))
    grad_attended = matmul(middle_half, out_rows.T)
    grad_att = by_head(halved(grad_attended))
    row_delta = jnp.sum(by_head(grad_attended) * widened(attended_heads), axis=-1, keepdims=True)
    grad_shares = jnp.einsum("hqd,hkd->hqk", grad_att, values, preferred_element_type=jnp.float32)
    grad_scores = halved(probs * (grad_shares - row_delta))
    grad_q = (
        jnp.einsum("hqk,hkd->hqd", grad_scores, keys, preferred_element_type=jnp.float32)
        * score_scale
    )
    grad_k = (
        jnp.einsum("hqk,hqd->hkd", grad_scores, queries, preferred_element_type=jnp.float32)
        * score_scale
    )
    grad_v = jnp.einsum("hqk,hqd->hkd", shares, grad_att, preferred_element_type=jnp.float32)
    grad_qkv = jnp.concatenate([by_token(grad_q), by_token(grad_k), by_token(grad_v)], axis=1)
    qkv_half = halved(grad_qkv)
    back_one = halved(matmul(qkv_half, qkv_cols.T)).reshape(n, tok_rows, D)
    d_qkv = by_core(matmul(normed_one.T, qkv_half))
    sums = jnp.sum(grad_qkv, axis=0)
    d_qv = jnp.stack([sums[:wide], sums[2 * wide :]])[:, None]
    back_one_got, d_proj_parts, d_fc_parts, d_qkv_got, d_out_got = run(
        5, greet_near, Exchange(back_one), Plane(d_proj), Plane(d_fc), Partner(d_qkv), Partner(d_out)
    )
    proj_grad = total(d_proj, d_proj_parts, chip)
    fc_rows = halved(total(d_fc, d_fc_parts, chip)).reshape(n, rows, dpc * units)
    d_qkv, d_out = pair(d_qkv, d_qkv_got), pair(d_out, d_out_got)
    _, norm_back_one = jax.vjp(layer_norm, stream, gain_one, bias_one)
    stream_branch, d_ln1_gain, d_ln1_bias = norm_back_one(total(back_one, back_one_got, s))
    grad_stream = grad_middle + stream_branch
    turn = jnp.arange(n, dtype=jnp.int32)[None, :, None] == s
    vectors = jnp.concatenate(
        [
            v.reshape(ranks, rows)
            for v in (d_ln1_gain, d_ln1_bias, d_out_bias, d_ln2_gain, d_ln2_bias, d_proj_bias)
        ]
        + [
            jnp.where(turn, d_qv, 0.0).reshape(ranks, -1),
            jnp.where(turn, d_fc_bias, 0.0).reshape(ranks, units),
        ],
        axis=1,
    )
    used = vectors.shape[1]
    vectors = jnp.pad(vectors, ((0, 0), (0, -used % 128))).reshape(ranks, -1, 128)
    d_qkv_parts, d_out_parts, fc_got, vectors_got, ff_got = run(
        6, greet_all, Plane(d_qkv), Plane(d_out), Exchange(fc_rows), Everyone(vectors), Exchange(ff_part)
    )
    output = middle + total(ff_part, ff_got, s) + proj_bias_full
    fc_grad = (
        widened(fill(fc_rows, fc_got, s))
        .reshape(n, rows, dpc, units)
        .transpose(1, 2, 0, 3)
        .reshape(rows, FF)
    )
    qkv_rows = halved(total(d_qkv, d_qkv_parts, chip)).reshape(n, rows, 3 * wide)
    out_grad_rows = halved(total(d_out, d_out_parts, chip))
    vector = jnp.sum(fill(vectors, vectors_got, dp * n + s), axis=0).reshape(-1)
    firsts = [vector[i * rows : (i + 1) * rows] for i in range(6)]
    at = 6 * rows
    qv_grad = vector[at : at + qv_bias.shape[0]]
    at += qv_bias.shape[0]
    fc_bias_grad = vector[at : at + units]
    qkv_got, out_grad = run(7, greet_all, Exchange(qkv_rows), Turn(out_grad_rows, True))
    qkv_grad = (
        widened(fill(qkv_rows, qkv_got, s))
        .reshape(n, rows, 3, wide)
        .transpose(1, 2, 0, 3)
        .reshape(rows, 3 * D)
    )
    return (
        output,
        grad_stream,
        firsts[0],
        firsts[1],
        qkv_grad,
        qv_grad,
        widened(out_grad),
        firsts[2],
        firsts[3],
        firsts[4],
        fc_grad,
        fc_bias_grad,
        proj_grad,
        firsts[5],
    )


def solution(mesh):
    in_specs = (
        P(("dp", "seq"), None),
        P(("dp", "seq"), None),
        P(("dp", "seq")),
        P(("dp", "seq")),
        P(("dp", "seq"), None),
        P(("dp", "seq")),
        P(("dp", "seq"), None),
        P(("dp", "seq")),
        P(("dp", "seq")),
        P(("dp", "seq")),
        P(("dp", "seq"), None),
        P(("dp", "seq")),
        P(("dp", "seq"), None),
        P(("dp", "seq")),
    )
    out_specs = (
        P(("dp", "seq"), None),
        P(("dp", "seq"), None),
        P(("dp", "seq")),
        P(("dp", "seq")),
        P(("dp", "seq"), None),
        P(("dp", "seq")),
        P(("dp", "seq"), None),
        P(("dp", "seq")),
        P(("dp", "seq")),
        P(("dp", "seq")),
        P(("dp", "seq"), None),
        P(("dp", "seq")),
        P(("dp", "seq"), None),
        P(("dp", "seq")),
    )
    return jax.shard_map(local, mesh=mesh, in_specs=in_specs, out_specs=out_specs, check_vma=False)
```

profile of v0, /device:TPU:0, one launch (start us, length us, event | category | flops | bytes accessed | tf_op | source)
XLA Modules:
  0.0 318.4 jit_solution(11782777338338597402)
XLA Ops:
  0.7 5.4 %concatenate.12 = bf16[384]{0:T(512)(128)(2,1)S(1)} concatenate(bf16[32]{0:T(256)(128)(2,1)} %param.16, bf16[32]{0:T(256)(128)(2,1)} %param.17, bf16[32]{0:T(256)(128)(2,1)} %param.21, bf16[32]{0:T(256)(128)(2,1)} %param.22, bf16[32]{0:T(256)(128)(2,1)} %param.23, bf16[32]{0:T(256)(128)(2,1)} %param.27, bf16[64]{0:T(256)(128)(2,1)} %param.19, bf16[128]{0:T(256)(128)(2,1)} %param.25), dimensions={0} | concatenate | bytes 1536 | tf_op jit(solution)/shard_map/concatenate | solution.py:525
  6.3 1.1 reshape.526
  7.7 1.1 reshape.528
  9.0 0.8 pad_maximum_fusion.1.pack_in
  9.9 63.2 %shard_map.245 = (bf16[4,128,1024]{2,1,0:T(8,128)(2,1)}, bf16[4,128,1024]{2,1,0:T(8,128)(2,1)}, bf16[8,4,32,1920]{3,2,1,0:T(8,128)(2,1)}, bf16[8,32,1024]{2,1,0:T(8,128)(2,1)}, bf16[8,128,1024]{2,1,0:T(8,128)(2,1)}) custom-call(bf16[128,1024]{1,0:T(8,128)(2,1)} %x_in.1, bf16[128,1024]{1,0:T(8,128)(2,1)} %g_in.1, ...), custom_call_target="tpu_custom_call" | custom-call | tf_op jit(solution)/shard_map/pallas_call | solution.py:466
  73.1 1.5 convert_reduce_fusion
  74.6 1.6 multiply_reduce_fusion
  76.2 1.0 slice.383
  78.1 0.5 fusion.18
  78.5 2.8 fusion.31
  81.9 4.5 %fusion.2 = f32[4,512,512]{1,2,0:T(8,128)} fusion(pred[512,512]{0,1:T(8,128)(4,1)S(1)} %iota_compare_fusion, bf16[4,512,64]{1,2,0:T(8,128)(2,1)S(1)} %bitcast.242, bf16[4,512,64]{1,2,0:T(8,128)(2,1)S(1)} %bitcast.244), kind=kOutput, calls=%fused_computation.3 | convolution fusion | flops 273680896 | bytes 4980736 | tf_op jit(solution)/shard_map/reduce_sum | solution.py:580
  86.4 2.7 convolution_convert_fusion.7
  89.2 0.7 copy-done.10
  89.9 1.4 convolution_convert_fusion.5
  91.3 25.2 %shard_map.246 = bf16[4,128,1024]{2,1,0:T(8,128)(2,1)} custom-call(bf16[4,128,1024]{2,1,0:T(8,128)(2,1)} %bitcast.203), custom_call_target="tpu_custom_call" | custom-call | tf_op jit(solution)/shard_map/pallas_call | solution.py:342
  116.5 1.6 fusion.84
  118.3 0.9 add_convert_fusion.1.refs_0_
  119.2 20.7 %shard_map.247 = bf16[4,128,1024]{2,1,0:T(8,128)(2,1)} custom-call(bf16[128,1024]{1,0:T(8,128)(2,1)} %add_convert_fusion.1.refs_0_), custom_call_target="tpu_custom_call" | custom-call | tf_op jit(solution)/shard_map/pallas_call | solution.py:342
  139.9 3.3 %fusion.24 = f32[512,1024]{1,0:T(8,128)S(1)} fusion(bf16[512,1024]{1,0:T(8,128)(2,1)} %bitcast.238, bf16[1024,1920]{1,0:T(8,128)(2,1)} %bitcast.250), kind=kOutput, calls=%fused_computation.36 | convolution fusion | flops 1073741824 | bytes 5242880 | tf_op jit(solution)/shard_map/dot_general | solution.py:45
  143.2 2.5 convolution_convert_fusion.4
  145.8 2.9 fusion.79
  148.6 1.8 convolution_convert_fusion.1
  150.5 1.6 copy.98
  152.1 1.2 copy-done.43
  153.4 2.3 fusion.27
  155.6 1.3 convolution_convert_fusion
  156.9 1.5 copy.97
  158.4 24.9 %shard_map.248 = bf16[4,128,1024]{2,1,0:T(8,128)(2,1)} custom-call(bf16[4,128,1024]{2,1,0:T(8,128)(2,1)} %bitcast.210), custom_call_target="tpu_custom_call" | custom-call | tf_op jit(solution)/shard_map/pallas_call | solution.py:342
  183.3 1.7 multiply_reduce_fusion.1
  185.5 0.8 fusion.77.refs_0_
  186.3 22.0 %shard_map.249 = (bf16[4,128,1024]{2,1,0:T(8,128)(2,1)}, bf16[4,128,1024]{2,1,0:T(8,128)(2,1)}, bf16[4,128,1024]{2,1,0:T(8,128)(2,1)}) custom-call(bf16[128,1024]{1,0:T(8,128)(2,1)} %fusion.77.refs_0_, bf16[2,4,128,1024]{3,2,1,0:T(8,128)(2,1)} %bitcast.200, bf16[2,4,128,1024]{3,2,1,0:T(8,128)(2,1)} %bitcast.201), custom_call_target="tpu_custom_call" | custom-call | tf_op jit(solution)/shard_map/pallas_call | solution.py:342
  208.3 2.7 fusion.13.refs_2_
  211.1 1.4 fusion.14.refs_1_
  212.5 0.5 fusion.93
  213.4 0.8 copy.100
  214.4 0.5 copy-done
  214.9 0.8 fusion.35
  215.8 0.8 multiply_convert_fusion
  216.8 0.8 convolution_multiply_fusion.1
  217.6 0.5 convolution_multiply_fusion
  218.1 3.6 %convolution_convert_fusion.3 = bf16[512,1024]{1,0:T(8,128)(2,1)} fusion(bf16[1024,1920]{1,0:T(8,128)(2,1)} %bitcast.251, f32[512,256]{0,1:T(8,128)S(1)} %bitcast.218, f32[512,256]{0,1:T(8,128)S(1)} %bitcast.227, f32[512,256]{0,1:T(8,128)S(1)} %bitcast.230), kind=kOutput, calls=%fused_computation.42 | convolution fusion | flops 808189952 | bytes 4194304 | tf_op jit(solution)/shard_map/dot_general | solution.py:45
  221.8 1.1 convolution_convert_fusion.2
  222.9 1.3 copy.99
  224.4 25.6 %shard_map.250 = (bf16[4,128,1024]{2,1,0:T(8,128)(2,1)}, bf16[4,128,1024]{2,1,0:T(8,128)(2,1)}, bf16[4,128,1024]{2,1,0:T(8,128)(2,1)}, bf16[4,128,768]{2,1,0:T(8,128)(2,1)}, bf16[4,32,1024]{2,1,0:T(8,128)(2,1)}) custom-call(bf16[4,128,1024]{2,1,0:T(8,128)(2,1)} %bitcast.206, bf16[4,128,1024]{2,1,0:T(8,128)(2,1)} %fusion.14.refs_1_, ...), custom_call_target="tpu_custom_call" | custom-call | tf_op jit(solution)/shard_map/pallas_call | solution.py:342
  250.0 2.5 add_bitcast_fusion
  252.5 0.5 fusion.45
  253.0 0.7 copy-done.4
  254.0 1.3 add_convert_fusion
  255.3 1.1 fusion.26.refs_0_
  256.4 0.8 fusion.57.refs_1_
  257.6 1.1 convert_reduce_fusion.2
  259.1 0.7 reshape.561.refs_3_
  259.7 35.4 %shard_map.251 = (bf16[4,128,768]{2,1,0:T(8,128)(2,1)}, bf16[4,32,1024]{2,1,0:T(8,128)(2,1)}, bf16[4,32,1024]{2,1,0:T(8,128)(2,1)}, f32[32,3,128]{2,1,0:T(4,128)}, bf16[4,128,1024]{2,1,0:T(8,128)(2,1)}) custom-call(bf16[4,128,768]{2,1,0:T(8,128)(2,1)} %fusion.26.refs_0_, bf16[4,32,1024]{2,1,0:T(8,128)(2,1)} %fusion.57.refs_1_, ...), custom_call_target="tpu_custom_call" | custom-call | tf_op jit(solution)/shard_map/pallas_call | solution.py:342
  295.2 1.7 fusion.68.refs_1_
  297.0 2.1 add_convert_fusion.2
  299.1 1.2 fusion.51
  300.4 0.6 slice.368
  301.0 0.5 slice_bitcast_fusion
  301.5 0.6 fusion.91
  302.1 11.5 %shard_map.252 = (bf16[4,32,768]{2,1,0:T(8,128)(2,1)}, bf16[32,1024]{1,0:T(8,128)(2,1)}) custom-call(bf16[4,32,768]{2,1,0:T(8,128)(2,1)} %bitcast.235, bf16[32,1024]{1,0:T(8,128)(2,1)} %fusion.68.refs_1_), custom_call_target="tpu_custom_call" | custom-call | tf_op jit(solution)/shard_map/pallas_call | solution.py:342
  313.6 1.0 select_convert_fusion.1
  315.3 1.0 reshape.604
  316.7 0.9 reshape.602
  317.7 0.7 convert_element_type.645
  (152 shorter events, 6.5 us)
Async XLA Ops:
  73.1 5.0 %copy-start.7 = (bf16[4,128,1024]{2,1,0:T(8,128)(2,1)S(1)}, bf16[4,128,1024]{2,1,0:T(8,128)(2,1)}, u32[]{:S(2)}) copy-start(bf16[4,128,1024]{2,1,0:T(8,128)(2,1)} %get-tuple-element.34) | copy-start | bytes 3145732
  78.5 2.8 copy-start.27
  81.6 4.8 %copy-start.33 = (bf16[512,256]{0,1:T(8,128)(2,1)}, bf16[512,256]{0,1:T(8,128)(2,1)S(1)}, u32[]{:S(2)}) copy-start(bf16[512,256]{0,1:T(8,128)(2,1)S(1)} %copy.61) | copy-start | bytes 786436
  81.8 4.6 %copy-start.35 = (bf16[512,256]{0,1:T(8,128)(2,1)}, bf16[512,256]{0,1:T(8,128)(2,1)S(1)}, u32[]{:S(2)}) copy-start(bf16[512,256]{0,1:T(8,128)(2,1)S(1)} %copy.62) | copy-start | bytes 786436
  81.9 4.5 %copy-start.21 = (bf16[512,256]{0,1:T(8,128)(2,1)}, bf16[512,256]{0,1:T(8,128)(2,1)S(1)}, u32[]{:S(2)}) copy-start(bf16[512,256]{0,1:T(8,128)(2,1)S(1)} %copy.63) | copy-start | bytes 786436
  86.4 3.4 %copy-start.23 = (bf16[8,32,1024]{2,1,0:T(8,128)(2,1)S(1)}, bf16[8,32,1024]{2,1,0:T(8,128)(2,1)}, u32[]{:S(2)}) copy-start(bf16[8,32,1024]{2,1,0:T(8,128)(2,1)} %get-tuple-element.36) | copy-start | bytes 1572868
  89.1 0.7 copy-start.10
  89.2 27.3 %copy-start.9 = (bf16[128,1024]{1,0:T(8,128)(2,1)S(1)}, bf16[128,1024]{1,0:T(8,128)(2,1)}, u32[]{:S(2)}) copy-start(bf16[128,1024]{1,0:T(8,128)(2,1)} %x_in.1) | copy-start | bytes 786436
  91.3 25.2 %copy-start.6 = (bf16[512,1024]{1,0:T(8,128)(2,1)S(1)}, bf16[512,1024]{1,0:T(8,128)(2,1)}, u32[]{:S(2)}) copy-start(bf16[512,1024]{1,0:T(8,128)(2,1)} %convolution_convert_fusion.5) | copy-start | bytes 3145732
  139.9 3.3 %copy-start.44 = (bf16[8,128,1024]{2,1,0:T(8,128)(2,1)S(1)}, bf16[8,128,1024]{2,1,0:T(8,128)(2,1)}, u32[]{:S(2)}) copy-start(bf16[8,128,1024]{2,1,0:T(8,128)(2,1)} %get-tuple-element.37) | copy-start | bytes 6291460
  143.2 2.5 copy-start.45
  150.5 2.9 copy-start.43
  153.3 2.3 copy-start.26
  158.4 24.9 %copy-start.15 = (bf16[512,1024]{1,0:T(8,128)(2,1)S(1)}, bf16[512,1024]{1,0:T(8,128)(2,1)}, u32[]{:S(2)}) copy-start(bf16[512,1024]{1,0:T(8,128)(2,1)} %fusion.27) | copy-start | bytes 3145732
  183.3 2.2 copy-start.19
  186.3 22.0 %copy-start.2 = (bf16[4,2,128,1024]{3,2,0,1:T(8,128)(2,1)S(1)}, bf16[4,2,128,1024]{3,2,0,1:T(8,128)(2,1)}, u32[]{:S(2)}) copy-start(bf16[4,2,128,1024]{3,2,0,1:T(8,128)(2,1)} %copy.97) | copy-start | bytes 6291460
  208.3 2.8 copy-start.1
  208.3 2.8 copy-start.31
  211.1 1.4 copy-start.14
  211.1 1.4 copy-start.24
  211.1 1.9 copy-start.11
  212.5 2.4 copy-start
  214.9 0.9 copy-start.22
  215.8 0.9 copy-start.34
  216.6 1.0 copy-start.36
  218.0 3.8 %copy-start.28 = (bf16[512,1024]{1,0:T(8,128)(2,1)S(1)}, bf16[512,1024]{1,0:T(8,128)(2,1)}, u32[]{:S(2)}) copy-start(bf16[512,1024]{1,0:T(8,128)(2,1)} %copy-done.27) | copy-start | bytes 3145732
  224.4 25.7 %copy-start.5 = (bf16[4,128,1024]{2,1,0:T(8,128)(2,1)S(1)}, bf16[4,128,1024]{2,1,0:T(8,128)(2,1)}, u32[]{:S(2)}) copy-start(bf16[4,128,1024]{2,1,0:T(8,128)(2,1)} %fusion.14.refs_1_) | copy-start | bytes 3145732
  250.0 2.5 copy-start.12
  250.0 2.5 copy-start.30
  252.5 1.2 copy-start.4
  252.5 1.5 copy-start.32
  252.5 2.8 copy-start.3
  252.5 2.8 copy-start.37
  254.0 2.4 copy-start.16
  254.0 2.4 copy-start.40
  255.3 2.3 copy-start.20
  257.6 37.7 %copy-start.17 = (bf16[4,32,1024]{2,1,0:T(8,128)(2,1)S(1)}, bf16[4,32,1024]{2,1,0:T(8,128)(2,1)}, u32[]{:S(2)}) copy-start(bf16[4,32,1024]{2,1,0:T(8,128)(2,1)} %fusion.57.refs_1_) | copy-start | bytes 786436
  258.7 38.2 %copy-start.8 = (bf16[4,128,768]{2,1,0:T(8,128)(2,1)S(1)}, bf16[4,128,768]{2,1,0:T(8,128)(2,1)}, u32[]{:S(2)}) copy-start(bf16[4,128,768]{2,1,0:T(8,128)(2,1)} %fusion.26.refs_0_) | copy-start | bytes 2359300
  259.7 39.3 %copy-start.13 = (bf16[512,1024]{1,0:T(8,128)(2,1)S(1)}, bf16[512,1024]{1,0:T(8,128)(2,1)}, u32[]{:S(2)}) copy-start(bf16[512,1024]{1,0:T(8,128)(2,1)} %convolution_convert_fusion.4) | copy-start | bytes 3145732
  295.2 3.9 %copy-start.29 = (bf16[4,128,1024]{2,1,0:T(8,128)(2,1)S(1)}, bf16[4,128,1024]{2,1,0:T(8,128)(2,1)}, u32[]{:S(2)}) copy-start(bf16[4,128,1024]{2,1,0:T(8,128)(2,1)} %get-tuple-element.46) | copy-start | bytes 3145732
  296.9 3.3 %copy-start.38 = (f32[32,3,128]{2,1,0:T(4,128)S(1)}, f32[32,3,128]{2,1,0:T(4,128)}, u32[]{:S(2)}) copy-start(f32[32,3,128]{2,1,0:T(4,128)} %reshape.561.refs_3_) | copy-start | bytes 147460
  296.9 3.3 %copy-start.42 = (f32[32,3,128]{2,1,0:T(4,128)S(1)}, f32[32,3,128]{2,1,0:T(4,128)}, u32[]{:S(2)}) copy-start(f32[32,3,128]{2,1,0:T(4,128)} %get-tuple-element.47) | copy-start | bytes 147460
  299.1 14.5 %copy-start.25 = (bf16[1,128,768]{2,1,0:T(8,128)(2,1)S(1)}, bf16[1,128,768]{2,1,0:T(8,128)(2,1)}, u32[]{:S(2)}) copy-start(bf16[1,128,768]{2,1,0:T(8,128)(2,1)} %add_convert_fusion.2) | copy-start | bytes 589828
  299.1 15.5 %copy-start.18 = (bf16[1,128,1024]{2,1,0:T(8,128)(2,1)S(1)}, bf16[1,128,1024]{2,1,0:T(8,128)(2,1)}, u32[]{:S(2)}) copy-start(bf16[1,128,1024]{2,1,0:T(8,128)(2,1)} %add_convert_fusion) | copy-start | bytes 786436
  299.1 15.5 %copy-start.39 = (bf16[4,32,1024]{2,1,0:T(8,128)(2,1)S(1)}, bf16[4,32,1024]{2,1,0:T(8,128)(2,1)}, u32[]{:S(2)}) copy-start(bf16[4,32,1024]{2,1,0:T(8,128)(2,1)} %get-tuple-element.52) | copy-start | bytes 786436
  315.2 2.4 copy-start.41
where the time goes:
time: 319 us; the launch traced here: 318 us
  Pallas kernels  228 us (71%)
  matrix products  33.8 us (11%)
  other arithmetic  29.3 us (9%)
  local copies, waits for them, and re-layouts  25.4 us (8%)
    pallas_call x7, Pallas kernels, run(): pl.pallas_call(kernel, out_shape=[jax.ShapeDtypeStruct(o.shape, o.dtype)...  165 us
    pallas_call x1, Pallas kernels, gather_inputs(): pl.pallas_call(kernel, out_shape=[grown(block_input, n), grown(cotangent,...  63.2 us
    dot_general x12, matrix products, matmul(): return jnp.dot(left, right, preferred_element_type=jnp.float32)  23.9 us
    convert_element_type x11, other arithmetic, halved(): return values.astype(jnp.bfloat16)  13.4 us

commit v1 on v0

v1 whole, which is shorter than its diff:
```python
import math

import jax
import jax.numpy as jnp
from jax import lax
from jax.experimental import pallas as pl
from jax.experimental.pallas import tpu as pltpu
from jax.sharding import PartitionSpec as P

D = 1024
H = 16
HD = 64
FF = 4096


EPS = 1e-05
GELU_COEF = math.sqrt(2.0 / math.pi)
MESH = pl.DeviceIdType.MESH


def layer_norm(values, norm_gain, offset):
    center = jnp.mean(values, axis=-1, keepdims=True)
    centred = values - center
    spread = jnp.mean(centred * centred, axis=-1, keepdims=True)
    return centred * lax.rsqrt(spread + EPS) * norm_gain + offset


def gelu_tanh(pre_act):
    return (
        0.5
        * pre_act
        * (1.0 + jnp.tanh(GELU_COEF * (pre_act + 0.044715 * pre_act * pre_act * pre_act)))
    )


def halved(values):
    return values.astype(jnp.bfloat16)


def widened(values):
    return values.astype(jnp.float32)


def matmul(left, right):
    return jnp.dot(left, right, preferred_element_type=jnp.float32)


def place():
    return lax.axis_index("dp"), lax.axis_index("seq")


def counts():
    return lax.axis_size("dp"), lax.axis_size("seq")


def remote(src, dst, send, recv, device):
    return pltpu.make_async_remote_copy(
        src_ref=src, dst_ref=dst, send_sem=send, recv_sem=recv, device_id=device, device_id_type=MESH
    )


def dma(*shape):
    return pltpu.SemaphoreType.DMA(shape)


def greet_all():
    dp, s = place()
    dpc, n = counts()
    barrier = pltpu.get_barrier_semaphore()

    def greet(i, carry):
        @pl.when(i != dp * n + s)
        def _():
            pl.semaphore_signal(barrier, inc=1, device_id=(i // n, i % n), device_id_type=MESH)

        return carry

    lax.fori_loop(0, dpc * n, greet, 0)
    pl.semaphore_wait(barrier, dpc * n - 1)


def greet_near():
    dp, s = place()
    dpc, n = counts()
    nc = dpc // 2
    barrier = pltpu.get_barrier_semaphore()
    for k in range(1, n):
        pl.semaphore_signal(barrier, inc=1, device_id=(dp, (s + k) % n), device_id_type=MESH)
    for k in range(1, nc):
        pl.semaphore_signal(barrier, inc=1, device_id=((dp + 2 * k) % dpc, s), device_id_type=MESH)
    pl.semaphore_signal(barrier, inc=1, device_id=(other_core(dp), s), device_id_type=MESH)
    pl.semaphore_wait(barrier, n - 1 + nc)


def greet_seq():
    dp, s = place()
    _, n = counts()
    barrier = pltpu.get_barrier_semaphore()
    for k in range(1, n):
        pl.semaphore_signal(barrier, inc=1, device_id=(dp, (s + k) % n), device_id_type=MESH)
    pl.semaphore_wait(barrier, n - 1)


def other_core(dp):
    return dp + 1 - 2 * (dp % 2)


class Exchange:
    def __init__(self, value):
        _, n = counts()
        self.operands = (value,)
        self.outs = (value,)
        self.sems = (dma(n), dma(n))

    def copies(self, ins, outs, sems):
        dp, s = place()
        _, n = counts()
        return [
            remote(
                ins[0].at[(s + k) % n], outs[0].at[s], sems[0].at[k], sems[1].at[k], (dp, (s + k) % n)
            )
            for k in range(n - 1, 0, -1)
        ]

    def start(self, ins, outs, sems):
        for copy in self.copies(ins, outs, sems):
            copy.start()

    def finish(self, ins, outs, sems):
        for copy in self.copies(ins, outs, sems):
            copy.wait()


class Plane(Exchange):
    def __init__(self, value):
        dpc, _ = counts()
        self.operands = (value,)
        self.outs = (value,)
        self.sems = (dma(dpc // 2), dma(dpc // 2))

    def copies(self, ins, outs, sems):
        dp, s = place()
        dpc, _ = counts()
        chip, core, nc = dp // 2, dp % 2, dpc // 2
        return [
            remote(
                ins[0].at[(chip + k) % nc],
                outs[0].at[chip],
                sems[0].at[k],
                sems[1].at[k],
                ((chip + k) % nc * 2 + core, s),
            )
            for k in range(1, nc)
        ]


class Partner(Exchange):
    def __init__(self, value):
        self.operands = (value,)
        self.outs = (jax.ShapeDtypeStruct(value.shape[1:], value.dtype),)
        self.sems = (dma(1), dma(1))

    def copies(self, ins, outs, sems):
        dp, s = place()
        return [
            remote(
                ins[0].at[1 - dp % 2], outs[0], sems[0].at[0], sems[1].at[0], (other_core(dp), s)
            )
        ]


class Everyone:
    def __init__(self, value):
        dpc, n = counts()
        self.operands = (value,)
        self.outs = (value,)
        self.sems = (dma(dpc * n), dma(dpc * n))

    def copy(self, ins, outs, sems, k):
        dp, s = place()
        dpc, n = counts()
        me = dp * n + s
        peer = (me + k) % (dpc * n)
        return remote(
            ins[0].at[peer], outs[0].at[me], sems[0].at[k], sems[1].at[k], (peer // n, peer % n)
        )

    def start(self, ins, outs, sems):
        def step(k, carry):
            self.copy(ins, outs, sems, k).start()
            return carry

        lax.fori_loop(1, self.outs[0].shape[0], step, 0)

    def finish(self, ins, outs, sems):
        def step(k, carry):
            self.copy(ins, outs, sems, k).wait()
            return carry

        lax.fori_loop(1, self.outs[0].shape[0], step, 0)


class Walk:
    def __init__(self, source, block, sems, pair=False, keep=True):
        self.source, self.block, self.sems, self.pair, self.keep = source, block, sems, pair, keep

    @staticmethod
    def scratch(pair=False):
        _, n = counts()
        return (dma(2, n), dma(2, n), dma(1)) + ((dma(2, n), dma(2, n)) if pair else ())

    def hand_on(self, way, k):
        dp, s = place()
        sign = 1 - 2 * way
        block = self.block(s - sign * k, dp % 2)
        return remote(
            self.source if k == 0 else block, block,
            self.sems[0].at[way, k], self.sems[1].at[way, k], (dp, s + sign),
        )

    def over(self, way, k, core):
        dp, s = place()
        block = self.block(s - (1 - 2 * way) * k, core)
        return remote(
            self.source if k == 0 else block, block,
            self.sems[3].at[way, k], self.sems[4].at[way, k], (other_core(dp), s),
        )

    def own(self):
        dp, s = place()
        return pltpu.make_async_copy(self.source, self.block(s, dp % 2), self.sems[2].at[0])

    def guard(self, way, k):
        _, s = place()
        _, n = counts()
        return (s >= k) if way == 0 else (s < n - k)

    def follows(self, way):
        _, s = place()
        _, n = counts()
        return (s < n - 1) if way == 0 else (s > 0)

    def start(self):
        dp, _ = place()
        for way in (0, 1):

            @pl.when(self.follows(way))
            def _():
                self.hand_on(way, 0).start()

        if self.keep:
            self.own().start()
        if self.pair:
            self.over(0, 0, dp % 2).start()

    def step(self, k):
        dp, s = place()
        _, n = counts()
        for way in (0, 1):
            sign = 1 - 2 * way

            @pl.when(self.guard(way, k))
            def _():
                block = self.block(s - sign * k, dp % 2)
                remote(
                    block, block, self.sems[0].at[way, k - 1], self.sems[1].at[way, k - 1],
                    (dp, s - sign),
                ).wait_recv()
                if k < n - 1:

                    @pl.when(self.follows(way))
                    def _():
                        self.hand_on(way, k).start()

                if self.pair:
                    self.over(way, k, dp % 2).start()

    def close(self):
        dp, _ = place()
        _, n = counts()
        for way in (0, 1):
            for k in range(n - 1):

                @pl.when(jnp.logical_and(self.follows(way), self.guard(way, k)))
                def _():
                    self.hand_on(way, k).wait_send()

        if self.keep:
            self.own().wait()
        if self.pair:
            self.over(0, 0, dp % 2).wait_send()
            self.over(0, 0, 1 - dp % 2).wait_recv()
            for way in (0, 1):
                for k in range(1, n):

                    @pl.when(self.guard(way, k))
                    def _():
                        self.over(way, k, dp % 2).wait_send()
                        self.over(way, k, 1 - dp % 2).wait_recv()


class Spread:
    def __init__(self, source, block, sems, pair=False):
        self.source, self.block, self.sems, self.pair = source, block, sems, pair

    @staticmethod
    def scratch(pair=False):
        dpc, _ = counts()
        nc = dpc // 2
        return (dma(nc), dma(nc)) + ((dma(nc), dma(nc)) if pair else ())

    def to_chips(self):
        dp, s = place()
        dpc, _ = counts()
        nc = dpc // 2
        return [
            remote(
                self.source, self.block(dp // 2, dp % 2), self.sems[0].at[k], self.sems[1].at[k],
                ((dp // 2 + k) % nc * 2 + dp % 2, s),
            )
            for k in range(1, nc)
        ]

    def over(self, k, core):
        dp, s = place()
        dpc, _ = counts()
        nc = dpc // 2
        block = self.block((dp // 2 - k + nc) % nc, core)
        return remote(
            self.source if k == 0 else block, block, self.sems[2].at[k], self.sems[3].at[k],
            (other_core(dp), s),
        )

    def start(self):
        dp, _ = place()
        for copy in self.to_chips():
            copy.start()
        if self.pair:
            self.over(0, dp % 2).start()

    def step(self):
        dp, s = place()
        dpc, _ = counts()
        nc = dpc // 2
        for k in range(1, nc):
            chip = (dp // 2 - k + nc) % nc
            block = self.block(chip, dp % 2)
            remote(
                block, block, self.sems[0].at[k], self.sems[1].at[k], (chip * 2 + dp % 2, s)
            ).wait_recv()
            if self.pair:
                self.over(k, dp % 2).start()

    def close(self):
        dp, _ = place()
        dpc, _ = counts()
        for copy in self.to_chips():
            copy.wait_send()
        if self.pair:
            for k in range(dpc // 2):
                self.over(k, dp % 2).wait_send()
                self.over(k, 1 - dp % 2).wait_recv()


class Gather:
    def __init__(self, value):
        dpc, _ = counts()
        self.operands = (value,)
        self.outs = (jax.ShapeDtypeStruct((dpc // 2,) + value.shape, value.dtype),)
        self.sems = Spread.scratch() + (dma(1),)

    def spread(self, ins, outs, sems):
        return Spread(ins[0], lambda chip, core: outs[0].at[chip], sems)

    def own(self, ins, outs, sems):
        dp, _ = place()
        return pltpu.make_async_copy(ins[0], outs[0].at[dp // 2], sems[2].at[0])

    def start(self, ins, outs, sems):
        self.spread(ins, outs, sems).start()
        self.own(ins, outs, sems).start()

    def finish(self, ins, outs, sems):
        self.spread(ins, outs, sems).step()
        self.spread(ins, outs, sems).close()
        self.own(ins, outs, sems).wait()


def run(number, greet, *tasks):
    spans = []
    a = b = c = 0
    for task in tasks:
        spans.append((a, b, c))
        a += len(task.operands)
        b += len(task.outs)
        c += len(task.sems)
    n_in, n_out = a, b

    def kernel(*refs):
        ins, outs, sems = refs[:n_in], refs[n_in : n_in + n_out], refs[n_in + n_out :]
        greet()
        views = [
            (
                ins[i : i + len(t.operands)],
                outs[o : o + len(t.outs)],
                sems[m : m + len(t.sems)],
            )
            for t, (i, o, m) in zip(tasks, spans)
        ]
        for t, view in zip(tasks, views):
            t.start(*view)
        for t, view in zip(tasks, views):
            t.finish(*view)

    return pl.pallas_call(
        kernel,
        out_shape=[jax.ShapeDtypeStruct(o.shape, o.dtype) for t in tasks for o in t.outs],
        in_specs=[pl.BlockSpec(memory_space=pl.ANY)] * n_in,
        out_specs=[pl.BlockSpec(memory_space=pl.ANY)] * n_out,
        scratch_shapes=[s for t in tasks for s in t.sems],
        compiler_params=pltpu.CompilerParams(collective_id=number, has_side_effects=True),
    )(*[v for t in tasks for v in t.operands])


def gather_inputs(block_input, cotangent, pack, small, out_rows, fc_rows, proj_rows):
    dpc, n = counts()
    nc = dpc // 2
    units = fc_rows.shape[1] // nc
    whole = pack.ndim == 2
    wide = block_input.shape[1] // n
    pieces = 3 if whole else 1
    rows = out_rows.shape[0]

    def kernel(
        x_in, g_in, pack_in, small_in, out_in, fc_in, proj_in,
        x_all, g_all, pack_all, small_all, out_all, fc_all, proj_all, fc_own, *sems,
    ):
        dp, s = place()
        chip, core = dp // 2, dp % 2

        def take(count):
            nonlocal sems
            head, sems = sems[:count], sems[count:]
            return head

        pack_send, pack_recv, small_send, small_recv, fc_send, fc_recv, local = take(7)
        x = Walk(x_in, lambda i, c: x_all.at[i], take(3))
        out = Walk(out_in, lambda i, c: out_all.at[dp, i], take(3))
        fc = Walk(fc_own, lambda i, c: fc_all.at[:, c, i], take(5), pair=True)
        proj = Walk(proj_in, lambda i, c: proj_all.at[c, i], take(5), pair=True)
        grads = Spread(g_in, lambda p, c: g_all.at[p], take(2))
        spread_pack = Spread(pack_all.at[dp], lambda p, c: pack_all.at[p * 2 + c], take(4), pair=True)
        spread_small = Spread(small_all.at[dp], lambda p, c: small_all.at[p * 2 + c], take(4), pair=True)
        spread_out = Spread(out_all.at[dp], lambda p, c: out_all.at[p * 2 + c], take(4), pair=True)

        def piece(to, j):
            if whole:
                source = pack_in.at[:, pl.ds(pl.multiple_of(j * n * wide + to * wide, 128), wide)]
                return source, pack_all.at[dp, s, :, pl.ds(j * wide, wide)]
            return pack_in.at[to], pack_all.at[dp, s]

        shuffles = []
        for k in range(n - 1, 0, -1):
            to = (s + k) % n
            for j in range(pieces):
                source, target = piece(to, j)
                shuffles.append(
                    remote(source, target, pack_send.at[j, k], pack_recv.at[j, k], (dp, to))
                )
            shuffles.append(
                remote(small_in, small_all.at[dp, s], small_send.at[k], small_recv.at[k], (dp, to))
            )

        def cut(to):
            return fc_in.at[:, pl.ds(pl.multiple_of(to * units, 128), units)]

        turns = [
            remote(
                cut((chip + k) % nc), fc_own.at[chip], fc_send.at[k], fc_recv.at[k],
                ((chip + k) % nc * 2 + core, s),
            )
            for k in range(1, nc)
        ]
        keeps = [
            pltpu.make_async_copy(*piece(s, j), local.at[j]) for j in range(pieces)
        ] + [
            pltpu.make_async_copy(small_in, small_all.at[dp, s], local.at[3]),
            pltpu.make_async_copy(cut(chip), fc_own.at[chip], local.at[4]),
        ]
        keep_g = pltpu.make_async_copy(g_in, g_all.at[chip], local.at[5])

        greet_near()
        for copy in shuffles + keeps:
            copy.start()
        x.start()
        out.start()
        for copy in turns:
            copy.start()
        for copy in shuffles + keeps:
            copy.wait()
        spread_pack.start()
        spread_small.start()
        grads.start()
        keep_g.start()
        for k in range(1, n):
            x.step(k)
            out.step(k)
        out.own().wait()
        spread_out.start()
        for copy in turns:
            copy.wait()
        fc.start()
        proj.start()
        spread_pack.step()
        spread_small.step()
        for k in range(1, n):
            fc.step(k)
            proj.step(k)
        spread_out.step()
        grads.step()
        x.close()
        out.keep = False
        out.close()
        fc.close()
        proj.close()
        for spread in (spread_pack, spread_small, spread_out, grads):
            spread.close()
        keep_g.wait()

    def grown(value, *lead):
        return jax.ShapeDtypeStruct(lead, value.dtype)

    depth = block_input.shape[1]
    return pl.pallas_call(
        kernel,
        out_shape=[
            grown(block_input, n, *block_input.shape), grown(cotangent, nc, *cotangent.shape),
            grown(pack, dpc, n, rows, 3 * wide), grown(small, dpc, n, *small.shape),
            grown(out_rows, dpc, n, *out_rows.shape), grown(fc_rows, nc, 2, n, rows, units),
            grown(proj_rows, 2, n, *proj_rows.shape), grown(fc_rows, nc, rows, units),
        ],
        in_specs=[pl.BlockSpec(memory_space=pl.ANY)] * 7,
        out_specs=[pl.BlockSpec(memory_space=pl.ANY)] * 8,
        scratch_shapes=[
            dma(pieces, n), dma(pieces, n), dma(n), dma(n), dma(nc), dma(nc), dma(6),
            *Walk.scratch(), *Walk.scratch(), *Walk.scratch(True), *Walk.scratch(True),
            *Spread.scratch(), *Spread.scratch(True), *Spread.scratch(True), *Spread.scratch(True),
        ],
        compiler_params=pltpu.CompilerParams(collective_id=0, has_side_effects=True),
    )(block_input, cotangent, pack, small, out_rows, fc_rows, proj_rows)[:7]


def total(own, received, mine):
    picked = [
        jnp.where(k == mine, widened(own[k]), widened(received[k])) for k in range(own.shape[0])
    ]
    result = picked[0]
    for value in picked[1:]:
        result = result + value
    return result


def fill(own, received, mine):
    slots = lax.broadcasted_iota(jnp.int32, (own.shape[0],) + (1,) * (own.ndim - 1), 0)
    return jnp.where(slots == mine, own, received)


def local(
    block_input, cotangent, ln1_gain, ln1_bias, qkv_weight, qv_bias, out_weight, out_bias, ln2_gain,
    ln2_bias, fc_weight, fc_bias, proj_weight, proj_bias,
):
    dp, s = place()
    dpc, n = counts()
    nc, ranks = dpc // 2, dpc * n
    core, chip = dp % 2, dp // 2
    tok_rows = block_input.shape[0]
    rows = qkv_weight.shape[0]
    own_units = fc_bias.shape[0]
    units = FF // nc
    heads = H // n
    wide = heads * HD
    length = n * tok_rows
    score_scale = HD ** (-0.5)

    def row_of(value, i):
        return jnp.pad(value[None], ((i, 15 - i), (0, 128 - value.shape[0])))

    parts = (ln1_gain, ln1_bias, out_bias, ln2_gain, ln2_bias, proj_bias, qv_bias, fc_bias)
    small = row_of(parts[0], 0)
    for i in range(1, 8):
        small = small + row_of(parts[i], i)
    pack = qkv_weight
    if wide % 128:
        pack = (
            qkv_weight.reshape(rows, 3, n, wide).transpose(2, 0, 1, 3).reshape(n, rows, 3 * wide)
        )
    x_all, g_all, pack_all, small_all, out_all, fc_all, proj_all = gather_inputs(
        block_input, cotangent, pack, small, out_weight, fc_weight, proj_weight
    )
    stream_seq = widened(x_all.reshape(length, D))
    grad_ff = g_all.reshape(nc * tok_rows, D)
    qkv_cols = pack_all.reshape(D, 3 * wide)
    out_full = out_all.reshape(D, D)
    fc_cols = fc_all.reshape(D, units)
    proj_rows = proj_all.reshape(units, D)
    smalls = small_all.reshape(ranks, 16, 128)
    gain_one, bias_one, out_bias_full, gain_two, bias_two, proj_bias_full = (
        widened(smalls[:, i, :rows].reshape(D)) for i in range(6)
    )
    qv_full = smalls[:, 6, : qv_bias.shape[0]].reshape(2, n, wide)
    qv_own = widened(lax.dynamic_index_in_dim(qv_full, s, 1, keepdims=False))
    fc_bias_cols = widened(
        lax.dynamic_index_in_dim(
            smalls[:, 7, :own_units].reshape(nc, units), chip, 0, keepdims=False
        )
    )

    normed_one = halved(layer_norm(stream_seq, gain_one, bias_one))
    projected = matmul(normed_one, qkv_cols)

    def by_head(values):
        return values.reshape(length, heads, HD).transpose(1, 0, 2)

    def by_token(values):
        return values.transpose(1, 0, 2).reshape(length, wide)

    def side_by_side(own, got):
        return fill(own, got, s).transpose(1, 0, 2).reshape(tok_rows, n * wide)

    queries = by_head(halved(projected[:, :wide] + qv_own[0]))
    keys = by_head(halved(projected[:, wide : 2 * wide]))
    values = by_head(halved(projected[:, 2 * wide :] + qv_own[1]))
    position = jnp.arange(length, dtype=jnp.int32)
    visible = position[None, :] <= position[:, None]
    scores = (
        jnp.einsum("hqd,hkd->hqk", queries, keys, preferred_element_type=jnp.float32) * score_scale
    )
    log_total = jnp.log(
        jnp.sum(jnp.where(visible, jnp.exp(scores), 0.0), axis=-1, keepdims=True)
    )
    probs = jnp.where(visible, jnp.exp(scores - log_total), 0.0)
    shares = halved(probs)
    attended_heads = halved(
        jnp.einsum("hqk,hkd->hqd", shares, values, preferred_element_type=jnp.float32)
    )
    attended = by_token(attended_heads).reshape(n, tok_rows, wide)
    (attended_got,) = run(1, greet_seq, Exchange(attended))
    attended_own = side_by_side(attended, attended_got)
    stream = widened(block_input)
    middle = stream + matmul(attended_own, out_full) + out_bias_full
    normed_two = halved(layer_norm(middle, gain_two, bias_two))
    (normed_all,) = run(2, greet_near, Gather(normed_two))
    normed_ff = normed_all.reshape(nc * tok_rows, D)
    grad_out = widened(cotangent)
    d_proj_bias = jnp.sum(grad_out, axis=0)
    pre_act = matmul(normed_ff, fc_cols) + fc_bias_cols
    hidden = halved(gelu_tanh(pre_act))
    grad_hidden = matmul(grad_ff, proj_rows.T)
    _, gelu_back = jax.vjp(gelu_tanh, pre_act)
    grad_pre = gelu_back(grad_hidden)[0]
    pre_half = halved(grad_pre)
    back_two = halved(matmul(pre_half, fc_cols.T)).reshape(nc, tok_rows, D)
    ff_part = halved(matmul(hidden, proj_rows)).reshape(nc, tok_rows, D)
    d_proj = halved(matmul(hidden.T, grad_ff)).reshape(2, n, own_units, D)
    d_fc = (
        halved(matmul(normed_ff.T, pre_half))
        .reshape(nc, 2, n, rows, units)
        .transpose(1, 2, 0, 3, 4)
    )
    d_fc_bias = jnp.sum(grad_pre, axis=0)
    back_two_got, d_proj_got, d_fc_got = run(
        3, greet_near, Plane(back_two), Partner(d_proj), Partner(d_fc)
    )

    def pair(own, received):
        kept = lax.dynamic_index_in_dim(own, core, 0, keepdims=False)
        return halved(widened(kept) + widened(received))

    _, norm_back_two = jax.vjp(layer_norm, middle, gain_two, bias_two)
    mid_branch, d_ln2_gain, d_ln2_bias = norm_back_two(total(back_two, back_two_got, chip))
    grad_middle = grad_out + mid_branch
    d_out_bias = jnp.sum(grad_middle, axis=0)
    middle_half = halved(grad_middle)
    d_out = (
        halved(matmul(attended_own.T, middle_half))
        .reshape(nc, 2, n * rows, D)
        .transpose(1, 0, 2, 3)
    )
    grad_attended = halved(matmul(middle_half, out_full.T))
    grad_attended = grad_attended.reshape(tok_rows, n, wide).transpose(1, 0, 2)
    d_proj, d_fc = pair(d_proj, d_proj_got), pair(d_fc, d_fc_got)
    grad_att_got, ff_got, d_proj_parts, d_out_got = run(
        4, greet_near, Exchange(grad_attended), Plane(ff_part), Exchange(d_proj), Partner(d_out)
    )
    proj_grad = total(d_proj, d_proj_parts, s)
    output = middle + total(ff_part, ff_got, chip) + proj_bias_full
    grad_att = by_head(fill(grad_attended, grad_att_got, s).reshape(length, wide))
    row_delta = jnp.sum(widened(grad_att) * widened(attended_heads), axis=-1, keepdims=True)
    grad_shares = jnp.einsum("hqd,hkd->hqk", grad_att, values, preferred_element_type=jnp.float32)
    grad_scores = halved(probs * (grad_shares - row_delta))
    grad_q = (
        jnp.einsum("hqk,hkd->hqd", grad_scores, keys, preferred_element_type=jnp.float32)
        * score_scale
    )
    grad_k = (
        jnp.einsum("hqk,hqd->hkd", grad_scores, queries, preferred_element_type=jnp.float32)
        * score_scale
    )
    grad_v = jnp.einsum("hqk,hqd->hkd", shares, grad_att, preferred_element_type=jnp.float32)
    grad_qkv = jnp.concatenate([by_token(grad_q), by_token(grad_k), by_token(grad_v)], axis=1)
    qkv_half = halved(grad_qkv)
    back_one = halved(matmul(qkv_half, qkv_cols.T)).reshape(n, tok_rows, D)
    d_qkv = (
        halved(matmul(normed_one.T, qkv_half))
        .reshape(nc, 2, n * rows, 3 * wide)
        .transpose(1, 0, 2, 3)
    )
    sums = jnp.sum(grad_qkv, axis=0)
    d_qv = jnp.stack([sums[:wide], sums[2 * wide :]])[:, None]
    d_out = pair(d_out, d_out_got)
    back_one_got, d_fc_parts, d_out_parts, d_qkv_got = run(
        5, greet_near, Exchange(back_one), Exchange(d_fc), Plane(d_out), Partner(d_qkv)
    )
    d_qkv = pair(d_qkv, d_qkv_got)
    fc_cut = halved(total(d_fc, d_fc_parts, s))
    out_cut = halved(total(d_out, d_out_parts, chip)).reshape(n, rows, D)
    _, norm_back_one = jax.vjp(layer_norm, stream, gain_one, bias_one)
    stream_branch, d_ln1_gain, d_ln1_bias = norm_back_one(total(back_one, back_one_got, s))
    grad_stream = grad_middle + stream_branch
    turn = jnp.arange(n, dtype=jnp.int32)[None, :, None] == s
    mine = jnp.arange(nc, dtype=jnp.int32)[:, None] == chip
    vectors = jnp.concatenate(
        [
            v.reshape(ranks, rows)
            for v in (d_ln1_gain, d_ln1_bias, d_out_bias, d_ln2_gain, d_ln2_bias, d_proj_bias)
        ]
        + [
            jnp.where(turn, d_qv, 0.0).reshape(ranks, -1),
            jnp.where(mine, d_fc_bias, 0.0).reshape(ranks, own_units),
        ],
        axis=1,
    )
    used = vectors.shape[1]
    vectors = jnp.pad(vectors, ((0, 0), (0, -used % 128))).reshape(ranks, -1, 128)
    d_qkv_parts, fc_got, d_out_last, vectors_got = run(
        6, greet_all, Plane(d_qkv), Plane(fc_cut), Exchange(out_cut), Everyone(vectors)
    )
    fc_grad = widened(fill(fc_cut, fc_got, chip)).transpose(1, 0, 2).reshape(rows, FF)
    out_grad = total(out_cut, d_out_last, s)
    qkv_rows = halved(total(d_qkv, d_qkv_parts, chip)).reshape(n, rows, 3 * wide)
    vector = jnp.sum(fill(vectors, vectors_got, dp * n + s), axis=0).reshape(-1)
    firsts = [vector[i * rows : (i + 1) * rows] for i in range(6)]
    at = 6 * rows
    qv_grad = vector[at : at + qv_bias.shape[0]]
    at += qv_bias.shape[0]
    fc_bias_grad = vector[at : at + own_units]
    (qkv_got,) = run(7, greet_seq, Exchange(qkv_rows))
    qkv_grad = (
        widened(fill(qkv_rows, qkv_got, s))
        .reshape(n, rows, 3, wide)
        .transpose(1, 2, 0, 3)
        .reshape(rows, 3 * D)
    )
    return (
        output, grad_stream, firsts[0], firsts[1], qkv_grad, qv_grad, out_grad, firsts[2],
        firsts[3], firsts[4], fc_grad, fc_bias_grad, proj_grad, firsts[5],
    )


def solution(mesh):
    in_specs = (
        P(("dp", "seq"), None),
        P(("dp", "seq"), None),
        P(("dp", "seq")),
        P(("dp", "seq")),
        P(("dp", "seq"), None),
        P(("dp", "seq")),
        P(("dp", "seq"), None),
        P(("dp", "seq")),
        P(("dp", "seq")),
        P(("dp", "seq")),
        P(("dp", "seq"), None),
        P(("dp", "seq")),
        P(("dp", "seq"), None),
        P(("dp", "seq")),
    )
    out_specs = (
        P(("dp", "seq"), None),
        P(("dp", "seq"), None),
        P(("dp", "seq")),
        P(("dp", "seq")),
        P(("dp", "seq"), None),
        P(("dp", "seq")),
        P(("dp", "seq"), None),
        P(("dp", "seq")),
        P(("dp", "seq")),
        P(("dp", "seq")),
        P(("dp", "seq"), None),
        P(("dp", "seq")),
        P(("dp", "seq"), None),
        P(("dp", "seq")),
    )
    return jax.shard_map(local, mesh=mesh, in_specs=in_specs, out_specs=out_specs, check_vma=False)
```

time: 319 us -> 319 us (level)
  Pallas kernels: 228 us -> 216 us
  matrix products: 33.8 us -> 43.2 us
  other arithmetic: 29.3 us -> 37.2 us
  local copies, waits for them, and re-layouts: 25.4 us -> 20.5 us
    pallas_call x7, Pallas kernels: 165 us -> 145 us  [run(): pl.pallas_call(kernel, out_shape=[jax.ShapeDtypeStruct(o.shape, o.dtype)...]
    pallas_call x1, Pallas kernels: 63.2 us -> 70.3 us  [gather_inputs(): pl.pallas_call(kernel, out_shape=[grown(block_input, n, *block_input.shap...]
    dot_general x12, matrix products: 23.9 us -> 29.9 us  [matmul(): return jnp.dot(left, right, preferred_element_type=jnp.float32)]
    concatenate x1 -> x0, local copies, waits for them, and re-layouts: 5.43 us -> none  [local(): jnp.concatenate([ln1_gain, ln1_bias, out_bias, ln2_gain, ln2_bias, proj_b...]
    reshape x15 -> x5, local copies, waits for them, and re-layouts: 9.4 us -> 5.96 us  [the longest x1 1.52 us: local(): d_fc = halved(matmul(normed_ff.T, pre_half)).reshape(nc, 2, n, rows, unit...]
where the time goes in v1:
time: 319 us; the launch traced here: 318 us
  Pallas kernels  216 us (68%)
  matrix products  43.2 us (14%)
  other arithmetic  37.2 us (12%)
  local copies, waits for them, and re-layouts  20.5 us (6%)
    pallas_call x7, Pallas kernels, run(): pl.pallas_call(kernel, out_shape=[jax.ShapeDtypeStruct(o.shape, o.dtype)...  145 us
    pallas_call x1, Pallas kernels, gather_inputs(): pl.pallas_call(kernel, out_shape=[grown(block_input, n, *block_input.shap...  70.3 us
    dot_general x12, matrix products, matmul(): return jnp.dot(left, right, preferred_element_type=jnp.float32)  29.9 us
    convert_element_type x11, other arithmetic, halved(): return values.astype(jnp.bfloat16)  13.1 us

profile of v1, /device:TPU:0, one launch (start us, length us, event | category | flops | bytes accessed | tf_op | source)
XLA Modules:
  0.0 318.1 jit_solution(11029279945809453766)
XLA Ops:
  0.6 1.4 pad_add_fusion.small_in
  2.0 70.3 %shard_map.245 = (bf16[4,128,1024]{2,1,0:T(8,128)(2,1)}, bf16[4,128,1024]{2,1,0:T(8,128)(2,1)}, bf16[8,4,32,768]{3,2,1,0:T(8,128)(2,1)}, bf16[8,4,16,128]{3,2,1,...) custom-call(bf16[128,1024]{1,0:T(8,128)(2,1)} %x_in.1, ...), custom_call_target="tpu_custom_call" | custom-call | tf_op jit(solution)/shard_map/pallas_call | solution.py:534
  72.4 1.6 fusion.60
  74.2 1.6 convert_reduce_fusion
  75.8 1.6 multiply_reduce_fusion
  77.9 1.0 fusion.89
  78.9 0.9 slice_reduce_fusion.1
  80.2 0.8 iota_compare_fusion
  81.3 5.6 %fusion.2 = f32[4,512,512]{1,2,0:T(8,128)} fusion(pred[512,512]{0,1:T(8,128)(4,1)} %iota_compare_fusion, bf16[4,512,64]{1,2,0:T(8,128)(2,1)S(1)} %bitcast.225, bf16[4,512,64]{1,2,0:T(8,128)(2,1)S(1)} %bitcast.227), kind=kOutput, calls=%fused_computation.3 | convolution fusion | flops 273680896 | bytes 4980736 | tf_op jit(solution)/shard_map/reduce_sum | solution.py:639
  86.9 2.7 convolution_convert_fusion.7
  89.7 0.9 copy.68.refs_0_
  90.5 9.9 %shard_map.246 = bf16[4,128,256]{2,1,0:T(8,128)(2,1)} custom-call(bf16[4,128,256]{2,1,0:T(8,128)(2,1)} %copy.68.refs_0_), custom_call_target="tpu_custom_call" | custom-call | tf_op jit(solution)/shard_map/pallas_call | solution.py:415
  100.5 1.1 select_bitcast_fusion
  101.8 2.2 fusion.88
  104.4 0.9 add_convert_fusion.3.refs_0_
  105.3 14.0 %shard_map.247 = bf16[4,128,1024]{2,1,0:T(8,128)(2,1)} custom-call(bf16[128,1024]{1,0:T(8,128)(2,1)} %add_convert_fusion.3.refs_0_), custom_call_target="tpu_custom_call" | custom-call | tf_op jit(solution)/shard_map/pallas_call | solution.py:415
  119.3 4.5 %fusion.90 = f32[512,1024]{1,0:T(8,128)} fusion(bf16[512,1024]{1,0:T(8,128)(2,1)} %bitcast.221, bf16[1024,1024]{1,0:T(8,128)(2,1)} %bitcast.251), kind=kOutput, calls=%fused_computation.180 | convolution fusion | flops 1073741824 | bytes 5242880 | tf_op jit(solution)/shard_map/dot_general | solution.py:45
  123.7 0.9 slice_reduce_fusion
  124.7 4.8 %convolution_convert_fusion.6 = bf16[512,1024]{1,0:T(8,128)(2,1)} fusion(bf16[1024,1024]{1,0:T(8,128)(2,1)} %bitcast.253, f32[512,1024]{1,0:T(8,128)} %fusion.90, f32[1024]{0:T(1024)S(1)} %bitcast.237), kind=kOutput, calls=%fused_computation.45 | convolution fusion | flops 1079508992 | bytes 5246976 | tf_op jit(solution)/shard_map/dot_general | solution.py:45
  129.6 5.4 %fusion.77 = (f32[1024]{0:T(1024)S(1)}, bf16[512,1024]{1,0:T(8,128)(2,1)S(1)}) fusion(f32[512,1024]{1,0:T(8,128)} %fusion.90, f32[1024]{0:T(1024)S(1)} %bitcast.238, bf16[512,1024]{1,0:T(8,128)(2,1)S(1)} %bitcast.257, bf16[1024,1024]{1,0:T(8,128)(2,1)} %bitcast.254), kind=kOutput, calls=%fused_computation.170 | convolution fusion | flops 1087372288 | bytes 6299648 | tf_op jit(solution)/shard_map/dot_general | solution.py:45
  135.0 2.3 convolution_convert_fusion.5
  137.3 3.0 convolution_convert_fusion.1
  140.3 1.3 convolution_convert_fusion
  141.7 1.5 copy.101
  143.2 14.9 %shard_map.248 = (bf16[4,128,1024]{2,1,0:T(8,128)(2,1)}, bf16[4,128,1024]{2,1,0:T(8,128)(2,1)}, bf16[4,4,32,1024]{3,2,1,0:T(8,128)(2,1)}) custom-call(bf16[4,128,1024]{2,1,0:T(8,128)(2,1)} %bitcast.199, bf16[2,4,128,1024]{3,2,1,0:T(8,128)(2,1)} %bitcast.195, bf16[2,4,4,32,1024]{4,3,2,1,0:T(8,128)(2,1)} %bitcast.189), custom_call_target="tpu_custom_call" | custom-call | tf_op jit(solution)/shard_map/pallas_call | solution.py:415
  158.2 1.8 multiply_reduce_fusion.1
  160.4 1.6 convolution_convert_fusion.8
  162.0 1.2 copy.72
  163.1 0.9 copy.73
  164.0 2.9 fusion.15.refs_2_
  166.9 0.8 convolution_convert_fusion.2
  167.7 1.5 copy.100
  169.2 32.1 %shard_map.249 = (bf16[4,128,256]{2,1,0:T(8,128)(2,1)}, bf16[4,128,1024]{2,1,0:T(8,128)(2,1)}, bf16[4,128,1024]{2,1,0:T(8,128)(2,1)}, bf16[4,128,1024]{2,1,0:T(8,128)(2,1)}) custom-call(bf16[4,128,256]{2,1,0:T(8,128)(2,1)} %bitcast.201, bf16[4,128,1024]{2,1,0:T(8,128)(2,1)} %bitcast.197, bf16[4,128,1024]{2,1,0:T(8,128)(2,1)} %fusion.15.refs_2_, ...), custom_call_target="tpu_custom_call" | custom-call | tf_op jit(solution)/shard_map/pallas_call | solution.py:415
  201.4 2.4 fusion.45
  204.3 3.1 fusion.27
  207.7 0.8 multiply_convert_fusion
  208.7 0.8 convolution_multiply_fusion.1
  210.1 1.0 copy-done.49
  211.1 2.0 convolution_convert_fusion.4
  213.1 1.4 fusion.14.refs_1_
  215.3 1.6 fusion.13.refs_2_
  217.4 1.1 convolution_convert_fusion.3
  218.5 1.3 copy.102
  219.8 47.9 %shard_map.250 = (bf16[4,128,1024]{2,1,0:T(8,128)(2,1)}, bf16[4,4,32,1024]{3,2,1,0:T(8,128)(2,1)}, bf16[4,128,1024]{2,1,0:T(8,128)(2,1)}, bf16[4,128,768]{2,1,0:T(8,128)(2,1)}) custom-call(bf16[4,128,1024]{2,1,0:T(8,128)(2,1)} %bitcast.198, bf16[4,4,32,1024]{3,2,1,0:T(8,128)(2,1)} %fusion.14.refs_1_, bf16[4,128,1024]{2,1,0:T(8,128)(2,1)} %fusion.13.refs_2_, ...), custom_call_target="tpu_custom_call" | custom-call | tf_op jit(solution)/shard_map/pallas_call | solution.py:415
  267.7 1.7 fusion.76
  269.9 1.1 convert_reduce_fusion.2
  271.4 1.6 fusion.25
  273.2 0.7 select_n.327
  274.5 0.7 bitcast_select_fusion
  275.1 0.8 concatenate.7
  276.0 0.7 reshape.554.refs_3_
  276.7 1.1 fusion.23.refs_0_
  278.1 1.1 fusion.55.refs_1_
  279.1 1.1 add_convert_fusion.1
  280.2 17.4 %shard_map.251 = (bf16[4,128,768]{2,1,0:T(8,128)(2,1)}, bf16[4,32,1024]{2,1,0:T(8,128)(2,1)}, bf16[4,32,1024]{2,1,0:T(8,128)(2,1)}, f32[32,3,128]{2,1,0:T(4,128)}) custom-call(bf16[4,128,768]{2,1,0:T(8,128)(2,1)} %fusion.23.refs_0_, bf16[4,32,1024]{2,1,0:T(8,128)(2,1)} %fusion.55.refs_1_, bf16[4,32,1024]{2,1,0:T(8,128)(2,1)} %bitcast.202, ...), custom_call_target="tpu_custom_call" | custom-call | tf_op jit(solution)/shard_map/pallas_call | solution.py:415
  297.6 0.9 select_reduce_fusion.1
  298.6 0.6 fusion.86
  299.2 2.1 add_convert_fusion.4
  301.3 9.1 %shard_map.252 = bf16[4,32,768]{2,1,0:T(8,128)(2,1)} custom-call(bf16[4,32,768]{2,1,0:T(8,128)(2,1)} %bitcast.218), custom_call_target="tpu_custom_call" | custom-call | tf_op jit(solution)/shard_map/pallas_call | solution.py:415
  310.4 1.2 select_convert_fusion
  312.1 0.9 reshape.589
  313.6 0.7 add_bitcast_fusion.1
  314.4 0.8 copy.93
  315.8 2.3 add_bitcast_fusion
  (159 shorter events, 8.9 us)
Async XLA Ops:
  72.3 5.1 %copy-start.1 = (bf16[4,128,1024]{2,1,0:T(8,128)(2,1)S(1)}, bf16[4,128,1024]{2,1,0:T(8,128)(2,1)}, u32[]{:S(2)}) copy-start(bf16[4,128,1024]{2,1,0:T(8,128)(2,1)} %get-tuple-element.36) | copy-start | bytes 3145732
  74.2 3.7 %copy-start.48 = (bf16[8,4,32,768]{3,2,1,0:T(8,128)(2,1)S(1)}, bf16[8,4,32,768]{3,2,1,0:T(8,128)(2,1)}, u32[]{:S(2)}) copy-start(bf16[8,4,32,768]{3,2,1,0:T(8,128)(2,1)} %get-tuple-element.38) | copy-start | bytes 4718596
  80.1 6.8 %copy-start.21 = (bf16[512,256]{0,1:T(8,128)(2,1)}, bf16[512,256]{0,1:T(8,128)(2,1)S(1)}, u32[]{:S(2)}) copy-start(bf16[512,256]{0,1:T(8,128)(2,1)S(1)} %copy.65) | copy-start | bytes 786436
  81.1 5.8 %copy-start.33 = (bf16[512,256]{0,1:T(8,128)(2,1)}, bf16[512,256]{0,1:T(8,128)(2,1)S(1)}, u32[]{:S(2)}) copy-start(bf16[512,256]{0,1:T(8,128)(2,1)S(1)} %copy.63) | copy-start | bytes 786436
  81.3 5.6 %copy-start.35 = (bf16[512,256]{0,1:T(8,128)(2,1)}, bf16[512,256]{0,1:T(8,128)(2,1)S(1)}, u32[]{:S(2)}) copy-start(bf16[512,256]{0,1:T(8,128)(2,1)S(1)} %copy.64) | copy-start | bytes 786436
  89.6 12.2 %copy-start.8 = (bf16[128,1024]{1,0:T(8,128)(2,1)S(1)}, bf16[128,1024]{1,0:T(8,128)(2,1)}, u32[]{:S(2)}) copy-start(bf16[128,1024]{1,0:T(8,128)(2,1)} %x_in.1) | copy-start | bytes 786436
  100.4 103.4 %copy-start.42 = (pred[4]{0:T(512)(128)(4,1)}, pred[4]{0:T(512)(128)(4,1)S(1)}, u32[]{:S(2)}) copy-start(pred[4]{0:T(512)(128)(4,1)S(1)} %iota_compare_fusion.3) | copy-start | bytes 16
  101.8 3.5 %copy-start.23 = (bf16[128,4,256]{0,2,1:T(8,128)(2,1)}, bf16[128,4,256]{0,2,1:T(8,128)(2,1)S(1)}, u32[]{:S(2)}) copy-start(bf16[128,4,256]{0,2,1:T(8,128)(2,1)S(1)} %copy.69) | copy-start | bytes 786436
  124.7 4.9 %copy-start.50 = (bf16[4,128,1024]{2,1,0:T(8,128)(2,1)S(1)}, bf16[4,128,1024]{2,1,0:T(8,128)(2,1)}, u32[]{:S(2)}) copy-start(bf16[4,128,1024]{2,1,0:T(8,128)(2,1)} %get-tuple-element.42) | copy-start | bytes 3145732
  129.6 5.4 %copy-start.47 = (bf16[4,2,4,32,1024]{4,3,2,1,0:T(8,128)(2,1)S(1)}, bf16[4,2,4,32,1024]{4,3,2,1,0:T(8,128)(2,1)}, u32[]{:S(2)}) copy-start(bf16[4,2,4,32,1024]{4,3,2,1,0:T(8,128)(2,1)} %get-tuple-element.40) | copy-start | bytes 6291460
  135.0 2.3 copy-start.51
  137.3 3.0 copy-start.28
  143.2 15.0 %copy-start.15 = (bf16[512,1024]{1,0:T(8,128)(2,1)S(1)}, bf16[512,1024]{1,0:T(8,128)(2,1)}, u32[]{:S(2)}) copy-start(bf16[512,1024]{1,0:T(8,128)(2,1)} %convolution_convert_fusion.5) | copy-start | bytes 3145732
  158.1 2.3 copy-start.9
  158.1 2.3 copy-start.16
  160.3 6.7 %copy-start.10 = (f32[128,1024]{1,0:T(8,128)}, f32[128,1024]{1,0:T(8,128)S(1)}, u32[]{:S(2)}) copy-start(f32[128,1024]{1,0:T(8,128)S(1)} %get-tuple-element.78) | copy-start | bytes 1572868
  162.0 5.0 %copy-start.24 = (bf16[128,4,256]{0,2,1:T(8,128)(2,1)S(1)}, bf16[128,4,256]{0,2,1:T(8,128)(2,1)}, u32[]{:S(2)}) copy-start(bf16[128,4,256]{0,2,1:T(8,128)(2,1)} %copy-done.23) | copy-start | bytes 786436
  169.2 32.2 %copy-start.13 = (bf16[512,1024]{1,0:T(8,128)(2,1)S(1)}, bf16[512,1024]{1,0:T(8,128)(2,1)}, u32[]{:S(2)}) copy-start(bf16[512,1024]{1,0:T(8,128)(2,1)} %convolution_convert_fusion.6) | copy-start | bytes 3145732
  201.4 2.4 copy-start.18
  201.4 2.4 copy-start.41
  204.2 3.5 %copy-start = (f32[4,512,512]{1,2,0:T(8,128)S(1)}, f32[4,512,512]{1,2,0:T(8,128)}, u32[]{:S(2)}) copy-start(f32[4,512,512]{1,2,0:T(8,128)} %fusion.2) | copy-start | bytes 12582916
  204.3 3.5 %copy-start.22 = (bf16[512,256]{0,1:T(8,128)(2,1)S(1)}, bf16[512,256]{0,1:T(8,128)(2,1)}, u32[]{:S(2)}) copy-start(bf16[512,256]{0,1:T(8,128)(2,1)} %copy-done.21) | copy-start | bytes 786436
  207.4 10.0 %copy-start.25 = (f32[4,512,64]{1,2,0:T(8,128)}, f32[4,512,64]{1,2,0:T(8,128)S(1)}, u32[]{:S(2)}) copy-start(f32[4,512,64]{1,2,0:T(8,128)S(1)} %fusion.27) | copy-start | bytes 1572868
  207.7 0.9 copy-start.34
  208.7 0.9 copy-start.36
  209.4 8.0 %copy-start.26 = (f32[4,512,64]{1,2,0:T(8,128)}, f32[4,512,64]{1,2,0:T(8,128)S(1)}, u32[]{:S(2)}) copy-start(f32[4,512,64]{1,2,0:T(8,128)S(1)} %convolution_multiply_fusion.1) | copy-start | bytes 1572868
  209.4 1.6 copy-start.49
  210.1 7.3 %copy-start.27 = (f32[4,512,64]{1,2,0:T(8,128)}, f32[4,512,64]{1,2,0:T(8,128)S(1)}, u32[]{:S(2)}) copy-start(f32[4,512,64]{1,2,0:T(8,128)S(1)} %convolution_multiply_fusion) | copy-start | bytes 1572868
  211.1 2.0 copy-start.2
  211.1 2.0 copy-start.29
  213.1 2.0 copy-start.3
  213.1 2.2 copy-start.30
  219.8 48.0 %copy-start.14 = (bf16[512,1024]{1,0:T(8,128)(2,1)S(1)}, bf16[512,1024]{1,0:T(8,128)(2,1)}, u32[]{:S(2)}) copy-start(bf16[512,1024]{1,0:T(8,128)(2,1)} %convolution_convert_fusion.4) | copy-start | bytes 3145732
  267.7 2.2 copy-start.11
  267.7 2.2 copy-start.17
  269.8 3.3 %copy-start.43 = (pred[4]{0:T(512)(128)(4,1)S(1)}, pred[4]{0:T(512)(128)(4,1)}, u32[]{:S(2)}) copy-start(pred[4]{0:T(512)(128)(4,1)} %copy-done.42) | copy-start | bytes 16
  269.9 6.8 %copy-start.4 = (bf16[4,2,128,768]{3,2,0,1:T(8,128)(2,1)S(1)}, bf16[4,2,128,768]{3,2,0,1:T(8,128)(2,1)}, u32[]{:S(2)}) copy-start(bf16[4,2,128,768]{3,2,0,1:T(8,128)(2,1)} %copy.102) | copy-start | bytes 4718596
  271.0 5.6 %copy-start.37 = (bf16[4,128,768]{2,1,0:T(8,128)(2,1)S(1)}, bf16[4,128,768]{2,1,0:T(8,128)(2,1)}, u32[]{:S(2)}) copy-start(bf16[4,128,768]{2,1,0:T(8,128)(2,1)} %get-tuple-element.50) | copy-start | bytes 2359300
  271.4 6.3 %copy-start.7 = (bf16[4,4,32,1024]{3,2,1,0:T(8,128)(2,1)S(1)}, bf16[4,4,32,1024]{3,2,1,0:T(8,128)(2,1)}, u32[]{:S(2)}) copy-start(bf16[4,4,32,1024]{3,2,1,0:T(8,128)(2,1)} %fusion.14.refs_1_) | copy-start | bytes 3145732
  273.9 0.6 copy-start.45
  276.6 1.4 copy-start.32
  276.6 2.5 copy-start.6
  276.6 2.5 copy-start.31
  279.1 18.5 %copy-start.38 = (f32[32,3,128]{2,1,0:T(4,128)S(1)}, f32[32,3,128]{2,1,0:T(4,128)}, u32[]{:S(2)}) copy-start(f32[32,3,128]{2,1,0:T(4,128)} %reshape.554.refs_3_) | copy-start | bytes 147460
  279.1 20.0 %copy-start.12 = (bf16[4,128,768]{2,1,0:T(8,128)(2,1)S(1)}, bf16[4,128,768]{2,1,0:T(8,128)(2,1)}, u32[]{:S(2)}) copy-start(bf16[4,128,768]{2,1,0:T(8,128)(2,1)} %fusion.23.refs_0_) | copy-start | bytes 2359300
  280.2 30.1 %copy-start.44 = (pred[4]{0:T(512)(128)(4,1)S(1)}, pred[4]{0:T(512)(128)(4,1)}, u32[]{:S(2)}) copy-start(pred[4]{0:T(512)(128)(4,1)} %copy-done.42) | copy-start | bytes 16
  301.3 12.3 %copy-start.19 = (bf16[1,128,1024]{2,1,0:T(8,128)(2,1)S(1)}, bf16[1,128,1024]{2,1,0:T(8,128)(2,1)}, u32[]{:S(2)}) copy-start(bf16[1,128,1024]{2,1,0:T(8,128)(2,1)} %add_convert_fusion.1) | copy-start | bytes 786436
  301.3 12.3 %copy-start.39 = (bf16[4,32,1024]{2,1,0:T(8,128)(2,1)S(1)}, bf16[4,32,1024]{2,1,0:T(8,128)(2,1)}, u32[]{:S(2)}) copy-start(bf16[4,32,1024]{2,1,0:T(8,128)(2,1)} %get-tuple-element.55) | copy-start | bytes 786436
  310.3 4.0 %copy-start.20 = (bf16[4,32,1024]{2,1,0:T(8,128)(2,1)S(1)}, bf16[4,32,1024]{2,1,0:T(8,128)(2,1)}, u32[]{:S(2)}) copy-start(bf16[4,32,1024]{2,1,0:T(8,128)(2,1)} %fusion.55.refs_1_) | copy-start | bytes 786436
  310.4 4.0 %copy-start.40 = (bf16[4,32,1024]{2,1,0:T(8,128)(2,1)S(1)}, bf16[4,32,1024]{2,1,0:T(8,128)(2,1)}, u32[]{:S(2)}) copy-start(bf16[4,32,1024]{2,1,0:T(8,128)(2,1)} %get-tuple-element.56) | copy-start | bytes 786436
  310.4 4.0 %copy-start.46 = (pred[4]{0:T(512)(128)(4,1)S(1)}, pred[4]{0:T(512)(128)(4,1)}, u32[]{:S(2)}) copy-start(pred[4]{0:T(512)(128)(4,1)} %copy-done.45) | copy-start | bytes 16
  311.8 4.0 %copy-start.5 = (bf16[4,128,1024]{2,1,0:T(8,128)(2,1)S(1)}, bf16[4,128,1024]{2,1,0:T(8,128)(2,1)}, u32[]{:S(2)}) copy-start(bf16[4,128,1024]{2,1,0:T(8,128)(2,1)} %fusion.15.refs_2_) | copy-start | bytes 3145732

commit v2 on v1

--- a/solution.py
+++ b/solution.py
@@ -565,7 +565,300 @@
     return jnp.where(slots == mine, own, received)
 
 
-def local(
+def mask_of(half, shape):
+    lane = lax.broadcasted_iota(jnp.int32, shape, len(shape) - 1)
+    return (lane // HD) % 2 == half
+
+
+def contract(left, right, dims):
+    return lax.dot_general(
+        left, right, ((dims[:1], dims[1:]), ((), ())), preferred_element_type=jnp.float32
+    )
+
+
+def unit_rows(values):
+    center = jnp.mean(values, axis=-1, keepdims=True)
+    centred = values - center
+    spread = jnp.mean(centred * centred, axis=-1, keepdims=True)
+    return centred, lax.rsqrt(spread + EPS)
+
+
+def part(ref, i, size):
+    return ref.at[pl.ds(pl.multiple_of(i * size, size), size)]
+
+
+def lanes(ref, i, size):
+    return ref.at[:, pl.ds(pl.multiple_of(i * size, size), size)]
+
+
+def softmax_block(q_masked, k, log_total, diagonal):
+    scores = contract(q_masked, k, (1, 1)) * HD ** (-0.5)
+    row = lax.broadcasted_iota(jnp.int32, scores.shape, 0) + diagonal
+    visible = lax.broadcasted_iota(jnp.int32, scores.shape, 1) <= row
+    if log_total is None:
+        log_total = jnp.log(
+            jnp.sum(jnp.where(visible, jnp.exp(scores), 0.0), axis=-1, keepdims=True)
+        )
+    return jnp.where(visible, jnp.exp(scores - log_total), 0.0), log_total
+
+
+def forward(block_input, cotangent, qkv_weight, small, out_weight, fc_weight, proj_weight):
+    dpc, n = counts()
+    nc, ranks = dpc // 2, dpc * n
+    tok, depth = block_input.shape
+    rows, units, own_units = out_weight.shape[0], fc_weight.shape[1] // nc, proj_weight.shape[0]
+    wide, length = depth // n, n * tok
+    heads = wide // HD
+    bias_own = 2 * depth // ranks
+
+    def kernel(*refs):
+        refs = list(refs)
+
+        def take(count):
+            head = refs[:count]
+            del refs[:count]
+            return head
+
+        x_in, g_in, qkv_in, small_in, out_in, fc_in, proj_in = take(7)
+        (
+            nv_o, g_o, wf_o, wp_o, fc_own, wq_o, wo_o, xn_o, qkv_o, att_o, atto_o, mid_o, par_o,
+            fcb_o, lt_o,
+        ) = take(15)
+        xv, xn, wq, wo, sm, qkv, att, atto, mid, n2, par, qvb, fcb, lt = take(14)
+        (
+            pack_send, pack_recv, small_send, small_recv, fc_send, fc_recv, local, att_send,
+            att_recv, save,
+        ) = take(10)
+        dp, s = place()
+        chip, core = dp // 2, dp % 2
+        me = dp * n + s
+
+        x = Walk(x_in, lambda i, c: part(xv, i, tok), take(3))
+        out = Walk(out_in, lambda i, c: part(wo, dp * n + i, rows), take(3))
+        fc = Walk(fc_own, lambda i, c: wf_o.at[:, c, i], take(5), pair=True)
+        proj = Walk(proj_in, lambda i, c: wp_o.at[c, i], take(5), pair=True)
+        grads = Spread(g_in, lambda p, c: g_o.at[p], take(2))
+
+        def strip(ref, size):
+            return lambda p, c: part(ref, p * 2 + c, size)
+
+        spread_pack = Spread(part(wq, dp, n * rows), strip(wq, n * rows), take(4), pair=True)
+        spread_small = Spread(part(sm, dp, n * 16), strip(sm, n * 16), take(4), pair=True)
+        spread_out = Spread(part(wo, dp, n * rows), strip(wo, n * rows), take(4), pair=True)
+        normed = Spread(n2, lambda p, c: nv_o.at[p], take(2))
+
+        def piece(to, j):
+            return (
+                qkv_in.at[:, pl.ds(pl.multiple_of(j * depth + to * wide, 128), wide)],
+                part(wq, me, rows).at[:, pl.ds(j * wide, wide)],
+            )
+
+        shuffles = []
+        for k in range(n - 1, 0, -1):
+            to = (s + k) % n
+            for j in range(3):
+                source, target = piece(to, j)
+                shuffles.append(
+                    remote(source, target, pack_send.at[j, k], pack_recv.at[j, k], (dp, to))
+                )
+            shuffles.append(
+                remote(small_in, part(sm, me, 16), small_send.at[k], small_recv.at[k], (dp, to))
+            )
+
+        turns = [
+            remote(
+                lanes(fc_in, (chip + k) % nc, units), fc_own.at[chip], fc_send.at[k], fc_recv.at[k],
+                ((chip + k) % nc * 2 + core, s),
+            )
+            for k in range(1, nc)
+        ]
+        keeps = [pltpu.make_async_copy(*piece(s, j), local.at[j]) for j in range(3)] + [
+            pltpu.make_async_copy(small_in, part(sm, me, 16), local.at[3]),
+            pltpu.make_async_copy(lanes(fc_in, chip, units), fc_own.at[chip], local.at[4]),
+        ]
+        keep_g = pltpu.make_async_copy(g_in, g_o.at[chip], local.at[5])
+
+        greet_near()
+        for copy in shuffles + keeps:
+            copy.start()
+        x.start()
+        out.start()
+        for copy in turns:
+            copy.start()
+        for copy in shuffles + keeps:
+            copy.wait()
+        spread_pack.start()
+        spread_small.start()
+        x.step(1)
+        out.step(1)
+        spread_small.step()
+        spread_small.close()
+        for size, target, width, at in (
+            (rows, par, depth, 0), (bias_own, qvb, 2 * depth, 6), (own_units, fcb, FF, 7)
+        ):
+            group = 128 // size
+            for j in range(width // 128):
+                total_tile = widened(sm[pl.ds(j * group * 16, 16)])
+                for r in range(1, group):
+                    tile = widened(sm[pl.ds((j * group + r) * 16, 16)])
+                    total_tile = total_tile + pltpu.roll(tile, r * size, 1)
+                target[:, pl.ds(j * 128, 128)] = total_tile
+        for k in range(2, n):
+            x.step(k)
+            out.step(k)
+        out.own().wait()
+        out.keep = False
+        spread_out.start()
+        for copy in turns:
+            copy.wait()
+        fc.start()
+        proj.start()
+        grads.start()
+        keep_g.start()
+        spread_pack.step()
+        spread_pack.close()
+        x.close()
+        qv_rows = [
+            qvb[6:7, pl.ds(pl.multiple_of(j * depth + s * wide, 128), wide)] for j in range(2)
+        ]
+        shift = jnp.concatenate([qv_rows[0], jnp.zeros((1, wide), jnp.float32), qv_rows[1]], axis=1)
+
+        def project(i, carry):
+            at = pl.ds(pl.multiple_of(i * tok, tok), tok)
+            centred, scale = unit_rows(widened(xv[at]))
+            normed_one = halved(centred * scale * par[0:1] + par[1:2])
+            xn[at] = normed_one
+            qkv[at] = halved(matmul(normed_one, wq[...]) + shift)
+            return carry
+
+        lax.fori_loop(0, n, project, 0)
+        saves = [
+            pltpu.make_async_copy(a, b, save.at[i])
+            for i, (a, b) in enumerate(
+                ((wq, wq_o), (xn, xn_o), (qkv, qkv_o), (par, par_o), (fcb, fcb_o), (att, att_o),
+                 (lt, lt_o), (wo, wo_o), (atto, atto_o), (mid, mid_o))
+            )
+        ]
+        for copy in saves[:5]:
+            copy.start()
+
+        def att_copy(i):
+            k = (i - s + n) % n
+            return remote(
+                part(att, i, tok), lanes(atto, s, wide), att_send.at[k], att_recv.at[k], (dp, i)
+            )
+
+        for i in range(n - 1, -1, -1):
+            seen = (i + 1) * tok
+            here = pl.ds(i * tok, tok)
+            for p in range(wide // 128):
+                q2 = qkv[here, pl.ds(p * 128, 128)]
+                k2 = qkv[pl.ds(0, seen), pl.ds(wide + p * 128, 128)]
+                v2 = qkv[pl.ds(0, seen), pl.ds(2 * wide + p * 128, 128)]
+                outs = []
+                for h in range(2):
+                    probs, log_total = softmax_block(
+                        jnp.where(mask_of(h, q2.shape), q2, jnp.zeros_like(q2)), k2, None, i * tok
+                    )
+                    lt[2 * p + h, here] = log_total
+                    outs.append(matmul(halved(probs), v2))
+                att[here, pl.ds(p * 128, 128)] = halved(
+                    jnp.where(mask_of(0, outs[0].shape), outs[0], outs[1])
+                )
+
+            @pl.when(i != s)
+            def _():
+                att_copy(i).start()
+
+            @pl.when(i == s)
+            def _():
+                pltpu.make_async_copy(
+                    part(att, i, tok), lanes(atto, s, wide), local.at[6]
+                ).start()
+
+            if i == n - 1:
+                fc.step(1)
+            if i == 1:
+                proj.step(1)
+        for copy in saves[5:7]:
+            copy.start()
+        spread_out.step()
+        spread_out.close()
+        saves[7].start()
+        pltpu.make_async_copy(part(att, s, tok), lanes(atto, s, wide), local.at[6]).wait()
+        for k in range(1, n):
+            to = (s + k) % n
+            remote(
+                part(att, to, tok), lanes(atto, s, wide), att_send.at[k], att_recv.at[k], (dp, to)
+            ).wait_send()
+            back = (s - k + n) % n
+            remote(
+                part(att, s, tok), lanes(atto, back, wide), att_send.at[k], att_recv.at[k],
+                (dp, back),
+            ).wait_recv()
+        middle = widened(xv[pl.ds(pl.multiple_of(s * tok, tok), tok)]) + matmul(
+            atto[...], wo[...]
+        ) + par[2:3]
+        mid[...] = middle
+        centred, scale = unit_rows(middle)
+        n2[...] = halved(centred * scale * par[3:4] + par[4:5])
+        normed.start()
+        keep_n = pltpu.make_async_copy(n2, nv_o.at[chip], local.at[7])
+        keep_n.start()
+        for copy in saves[8:]:
+            copy.start()
+        for k in range(2, n):
+            fc.step(k)
+            proj.step(k)
+        grads.step()
+        normed.step()
+        out.close()
+        fc.close()
+        proj.close()
+        grads.close()
+        normed.close()
+        keep_g.wait()
+        keep_n.wait()
+        for copy in saves:
+            copy.wait()
+
+    half = jnp.bfloat16
+
+    def shape(kind, *dims):
+        return jax.ShapeDtypeStruct(dims, kind)
+
+    return pl.pallas_call(
+        kernel,
+        out_shape=[
+            shape(half, nc, tok, depth), shape(half, nc, tok, depth),
+            shape(half, nc, 2, n, rows, units), shape(half, 2, n, own_units, depth),
+            shape(half, nc, rows, units), shape(half, depth, 3 * wide), shape(half, depth, depth),
+            shape(half, length, depth), shape(half, length, 3 * wide), shape(half, length, wide),
+            shape(half, tok, depth), shape(jnp.float32, tok, depth), shape(jnp.float32, 16, depth),
+            shape(jnp.float32, 16, FF), shape(jnp.float32, heads, length, 1),
+        ],
+        in_specs=[pl.BlockSpec(memory_space=pl.ANY)] * 7,
+        out_specs=[pl.BlockSpec(memory_space=pl.ANY)] * 15,
+        scratch_shapes=[
+            pltpu.VMEM((length, depth), half), pltpu.VMEM((length, depth), half),
+            pltpu.VMEM((depth, 3 * wide), half), pltpu.VMEM((depth, depth), half),
+            pltpu.VMEM((ranks * 16, 128), half), pltpu.VMEM((length, 3 * wide), half),
+            pltpu.VMEM((length, wide), half), pltpu.VMEM((tok, depth), half),
+            pltpu.VMEM((tok, depth), jnp.float32), pltpu.VMEM((tok, depth), half),
+            pltpu.VMEM((16, depth), jnp.float32), pltpu.VMEM((16, 2 * depth), jnp.float32),
+            pltpu.VMEM((16, FF), jnp.float32), pltpu.VMEM((heads, length, 1), jnp.float32),
+            dma(3, n), dma(3, n), dma(n), dma(n), dma(nc), dma(nc), dma(8), dma(n), dma(n), dma(10),
+            *Walk.scratch(), *Walk.scratch(), *Walk.scratch(True), *Walk.scratch(True),
+            *Spread.scratch(), *Spread.scratch(True), *Spread.scratch(True), *Spread.scratch(True),
+            *Spread.scratch(),
+        ],
+        compiler_params=pltpu.CompilerParams(
+            collective_id=10, has_side_effects=True, vmem_limit_bytes=48 << 20
+        ),
+    )(block_input, cotangent, qkv_weight, small, out_weight, fc_weight, proj_weight)
+
+
+def plain(
     block_input, cotangent, ln1_gain, ln1_bias, qkv_weight, qv_bias, out_weight, out_bias, ln2_gain,
     ln2_bias, fc_weight, fc_bias, proj_weight, proj_bias,
 ):
@@ -767,6 +1060,183 @@
     )
 
 
+def fused(
+    block_input, cotangent, ln1_gain, ln1_bias, qkv_weight, qv_bias, out_weight, out_bias, ln2_gain,
+    ln2_bias, fc_weight, fc_bias, proj_weight, proj_bias,
+):
+    dp, s = place()
+    dpc, n = counts()
+    nc, ranks = dpc // 2, dpc * n
+    core, chip = dp % 2, dp // 2
+    tok_rows = block_input.shape[0]
+    rows = qkv_weight.shape[0]
+    own_units = fc_bias.shape[0]
+    units = FF // nc
+    heads = H // n
+    wide = heads * HD
+    length = n * tok_rows
+    score_scale = HD ** (-0.5)
+
+    def row_of(value, i):
+        return jnp.pad(value[None], ((i, 15 - i), (0, 128 - value.shape[0])))
+
+    parts = (ln1_gain, ln1_bias, out_bias, ln2_gain, ln2_bias, proj_bias, qv_bias, fc_bias)
+    small = row_of(parts[0], 0)
+    for i in range(1, 8):
+        small = small + row_of(parts[i], i)
+    (
+        normed_all, g_all, fc_all, proj_all, _, qkv_cols, out_full, xn_all, qkv, attended, attended_own,
+        middle, par, fcb, _,
+    ) = forward(block_input, cotangent, qkv_weight, small, out_weight, fc_weight, proj_weight)
+    grad_ff = g_all.reshape(nc * tok_rows, D)
+    fc_cols = fc_all.reshape(D, units)
+    proj_rows = proj_all.reshape(units, D)
+    gain_one, bias_one, out_bias_full, gain_two, bias_two, proj_bias_full = (par[i] for i in range(6))
+    fc_bias_cols = lax.dynamic_slice_in_dim(fcb[7], chip * units, units, 0)
+
+    def by_head(values):
+        return values.reshape(length, heads, HD).transpose(1, 0, 2)
+
+    def by_token(values):
+        return values.transpose(1, 0, 2).reshape(length, wide)
+
+    normed_one = xn_all
+    queries, keys, values = (by_head(qkv[:, i * wide : (i + 1) * wide]) for i in range(3))
+    attended_heads = by_head(attended)
+    position = jnp.arange(length, dtype=jnp.int32)
+    visible = position[None, :] <= position[:, None]
+    scores = (
+        jnp.einsum("hqd,hkd->hqk", queries, keys, preferred_element_type=jnp.float32) * score_scale
+    )
+    log_total = jnp.log(
+        jnp.sum(jnp.where(visible, jnp.exp(scores), 0.0), axis=-1, keepdims=True)
+    )
+    probs = jnp.where(visible, jnp.exp(scores - log_total), 0.0)
+    shares = halved(probs)
+    stream = widened(block_input)
+    normed_ff = normed_all.reshape(nc * tok_rows, D)
+    grad_out = widened(cotangent)
+    d_proj_bias = jnp.sum(grad_out, axis=0)
+    pre_act = matmul(normed_ff, fc_cols) + fc_bias_cols
+    hidden = halved(gelu_tanh(pre_act))
+    grad_hidden = matmul(grad_ff, proj_rows.T)
+    _, gelu_back = jax.vjp(gelu_tanh, pre_act)
+    grad_pre = gelu_back(grad_hidden)[0]
+    pre_half = halved(grad_pre)
+    back_two = halved(matmul(pre_half, fc_cols.T)).reshape(nc, tok_rows, D)
+    ff_part = halved(matmul(hidden, proj_rows)).reshape(nc, tok_rows, D)
+    d_proj = halved(matmul(hidden.T, grad_ff)).reshape(2, n, own_units, D)
+    d_fc = (
+        halved(matmul(normed_ff.T, pre_half))
+        .reshape(nc, 2, n, rows, units)
+        .transpose(1, 2, 0, 3, 4)
+    )
+    d_fc_bias = jnp.sum(grad_pre, axis=0)
+    back_two_got, d_proj_got, d_fc_got = run(
+        3, greet_near, Plane(back_two), Partner(d_proj), Partner(d_fc)
+    )
+
+    def pair(own, received):
+        kept = lax.dynamic_index_in_dim(own, core, 0, keepdims=False)
+        return halved(widened(kept) + widened(received))
+
+    _, norm_back_two = jax.vjp(layer_norm, middle, gain_two, bias_two)
+    mid_branch, d_ln2_gain, d_ln2_bias = norm_back_two(total(back_two, back_two_got, chip))
+    grad_middle = grad_out + mid_branch
+    d_out_bias = jnp.sum(grad_middle, axis=0)
+    middle_half = halved(grad_middle)
+    d_out = (
+        halved(matmul(attended_own.T, middle_half))
+        .reshape(nc, 2, n * rows, D)
+        .transpose(1, 0, 2, 3)
+    )
+    grad_attended = halved(matmul(middle_half, out_full.T))
+    grad_attended = grad_attended.reshape(tok_rows, n, wide).transpose(1, 0, 2)
+    d_proj, d_fc = pair(d_proj, d_proj_got), pair(d_fc, d_fc_got)
+    grad_att_got, ff_got, d_proj_parts, d_out_got = run(
+        4, greet_near, Exchange(grad_attended), Plane(ff_part), Exchange(d_proj), Partner(d_out)
+    )
+    proj_grad = total(d_proj, d_proj_parts, s)
+    output = middle + total(ff_part, ff_got, chip) + proj_bias_full
+    grad_att = by_head(fill(grad_attended, grad_att_got, s).reshape(length, wide))
+    row_delta = jnp.sum(widened(grad_att) * widened(attended_heads), axis=-1, keepdims=True)
+    grad_shares = jnp.einsum("hqd,hkd->hqk", grad_att, values, preferred_element_type=jnp.float32)
+    grad_scores = halved(probs * (grad_shares - row_delta))
+    grad_q = (
+        jnp.einsum("hqk,hkd->hqd", grad_scores, keys, preferred_element_type=jnp.float32)
+        * score_scale
+    )
+    grad_k = (
+        jnp.einsum("hqk,hqd->hkd", grad_scores, queries, preferred_element_type=jnp.float32)
+        * score_scale
+    )
+    grad_v = jnp.einsum("hqk,hqd->hkd", shares, grad_att, preferred_element_type=jnp.float32)
+    grad_qkv = jnp.concatenate([by_token(grad_q), by_token(grad_k), by_token(grad_v)], axis=1)
+    qkv_half = halved(grad_qkv)
+    back_one = halved(matmul(qkv_half, qkv_cols.T)).reshape(n, tok_rows, D)
+    d_qkv = (
+        halved(matmul(normed_one.T, qkv_half))
+        .reshape(nc, 2, n * rows, 3 * wide)
+        .transpose(1, 0, 2, 3)
+    )
+    sums = jnp.sum(grad_qkv, axis=0)
+    d_qv = jnp.stack([sums[:wide], sums[2 * wide :]])[:, None]
+    d_out = pair(d_out, d_out_got)
+    back_one_got, d_fc_parts, d_out_parts, d_qkv_got = run(
+        5, greet_near, Exchange(back_one), Exchange(d_fc), Plane(d_out), Partner(d_qkv)
+    )
+    d_qkv = pair(d_qkv, d_qkv_got)
+    fc_cut = halved(total(d_fc, d_fc_parts, s))
+    out_cut = halved(total(d_out, d_out_parts, chip)).reshape(n, rows, D)
+    _, norm_back_one = jax.vjp(layer_norm, stream, gain_one, bias_one)
+    stream_branch, d_ln1_gain, d_ln1_bias = norm_back_one(total(back_one, back_one_got, s))
+    grad_stream = grad_middle + stream_branch
+    turn = jnp.arange(n, dtype=jnp.int32)[None, :, None] == s
+    mine = jnp.arange(nc, dtype=jnp.int32)[:, None] == chip
+    vectors = jnp.concatenate(
+        [
+            v.reshape(ranks, rows)
+            for v in (d_ln1_gain, d_ln1_bias, d_out_bias, d_ln2_gain, d_ln2_bias, d_proj_bias)
+        ]
+        + [
+            jnp.where(turn, d_qv, 0.0).reshape(ranks, -1),
+            jnp.where(mine, d_fc_bias, 0.0).reshape(ranks, own_units),
+        ],
+        axis=1,
+    )
+    used = vectors.shape[1]
+    vectors = jnp.pad(vectors, ((0, 0), (0, -used % 128))).reshape(ranks, -1, 128)
+    d_qkv_parts, fc_got, d_out_last, vectors_got = run(
+        6, greet_all, Plane(d_qkv), Plane(fc_cut), Exchange(out_cut), Everyone(vectors)
+    )
+    fc_grad = widened(fill(fc_cut, fc_got, chip)).transpose(1, 0, 2).reshape(rows, FF)
+    out_grad = total(out_cut, d_out_last, s)
+    qkv_rows = halved(total(d_qkv, d_qkv_parts, chip)).reshape(n, rows, 3 * wide)
+    vector = jnp.sum(fill(vectors, vectors_got, dp * n + s), axis=0).reshape(-1)
+    firsts = [vector[i * rows : (i + 1) * rows] for i in range(6)]
+    at = 6 * rows
+    qv_grad = vector[at : at + qv_bias.shape[0]]
+    at += qv_bias.shape[0]
+    fc_bias_grad = vector[at : at + own_units]
+    (qkv_got,) = run(7, greet_seq, Exchange(qkv_rows))
+    qkv_grad = (
+        widened(fill(qkv_rows, qkv_got, s))
+        .reshape(n, rows, 3, wide)
+        .transpose(1, 2, 0, 3)
+        .reshape(rows, 3 * D)
+    )
+    return (
+        output, grad_stream, firsts[0], firsts[1], qkv_grad, qv_grad, out_grad, firsts[2],
+        firsts[3], firsts[4], fc_grad, fc_bias_grad, proj_grad, firsts[5],
+    )
+
+
+def local(*arrays):
+    _, n = counts()
+    fits = (D // n) % 128 == 0 and arrays[4].shape[0] % 16 == 0 and arrays[0].shape[0] % 128 == 0
+    return fused(*arrays) if fits else plain(*arrays)
+
+
 def solution(mesh):
     in_specs = (
         P(("dp", "seq"), None),

time: 319 us -> 280 us (0.88)
  Pallas kernels: 216 us -> 195 us
  matrix products: 43.2 us -> 29.3 us
  other arithmetic: 37.2 us -> 26.5 us
  local copies, waits for them, and re-layouts: 20.5 us -> 27 us
    pallas_call x7 -> x5, Pallas kernels: 145 us -> 122 us  [run(): pl.pallas_call(kernel, out_shape=[jax.ShapeDtypeStruct(o.shape, o.dtype)...]
    dot_general x12 -> x10, matrix products: 29.9 us -> 19.8 us  [matmul(): return jnp.dot(left, right, preferred_element_type=jnp.float32)]
    unnamed x104 -> x90, local copies, waits for them, and re-layouts: 3.36 us -> 10.7 us
    slice x9 -> x10, local copies, waits for them, and re-layouts: 3.68 us -> 7.03 us  [the longest x4 5.3 us: fused(): qkv[:, i * wide:(i + 1) * wide]]
    dot_general x5 -> x4, matrix products: 7.73 us -> 5.05 us  [the longest x1 3.09 us: fused(): jnp.einsum('hqk,hqd->hkd', shares, grad_att, preferred_element_type=jnp.f...]
    convert_element_type x11 -> x7, other arithmetic: 13.1 us -> 13.6 us  [halved(): return values.astype(jnp.bfloat16)]
where the time goes in v2:
time: 280 us; the launch traced here: 279 us
  Pallas kernels  195 us (70%)
  matrix products  29.3 us (10%)
  local copies, waits for them, and re-layouts  27 us (10%)
  other arithmetic  26.5 us (9%)
    pallas_call x5, Pallas kernels, run(): pl.pallas_call(kernel, out_shape=[jax.ShapeDtypeStruct(o.shape, o.dtype)...  122 us
    pallas_call x1, Pallas kernels, forward(): pl.pallas_call(kernel, out_shape=[shape(half, nc, tok, depth), shape(half...  73.1 us
    dot_general x10, matrix products, matmul(): return jnp.dot(left, right, preferred_element_type=jnp.float32)  19.8 us
    convert_element_type x7, other arithmetic, halved(): return values.astype(jnp.bfloat16)  13.6 us
    unnamed x90, local copies, waits for them, and re-layouts  10.7 us

profile of v2, /device:TPU:0, one launch (start us, length us, event | category | flops | bytes accessed | tf_op | source)
XLA Modules:
  0.0 279.2 jit_solution(3532283428580585564)
XLA Ops:
  0.9 1.1 convert_reduce_fusion
  2.0 0.8 pad_add_fusion.refs_3_
  2.8 0.8 iota_compare_fusion
  3.5 0.9 copy-done
  4.5 0.9 copy-done.2
  5.4 0.9 copy-done.4
  6.4 0.9 copy-done.5
  7.3 0.9 copy-done.6
  8.3 0.8 copy-done.7
  9.1 73.1 %shard_map.245 = (bf16[4,128,1024]{2,1,0:T(8,128)(2,1)S(1)}, bf16[4,128,1024]{2,1,0:T(8,128)(2,1)S(1)}, bf16[4,2,4,32,1024]{4,3,2,1,0:T(8,128)(2,1)}, bf16[2,4,1...) custom-call(bf16[128,1024]{1,0:T(8,128)(2,1)S(1)} %copy-done, ...), custom_call_target="tpu_custom_call" | custom-call | tf_op jit(solution)/shard_map/pallas_call | solution.py:830
  82.3 1.0 copy-done.8
  83.8 0.8 fusion.69
  84.7 1.8 copy.63
  86.5 1.8 copy.61
  88.3 0.8 copy.60
  89.1 3.0 %fusion.73 = f32[512,1024]{1,0:T(8,128)S(1)} fusion(bf16[512,1024]{1,0:T(8,128)(2,1)S(1)} %bitcast.165, bf16[1024,1024]{1,0:T(8,128)(2,1)} %bitcast.223), kind=kOutput, calls=%fused_computation.141 | convolution fusion | flops 1073741824 | bytes 5242880 | tf_op jit(solution)/shard_map/dot_general | solution.py:45
  92.1 2.5 convolution_convert_fusion.6
  94.6 2.9 %fusion.61 = (f32[1024]{0:T(1024)S(1)}, bf16[512,1024]{1,0:T(8,128)(2,1)S(1)}) fusion(f32[512,1024]{1,0:T(8,128)S(1)} %fusion.73, f32[1024]{0:T(1024)S(1)} %bitcast.210, bf16[512,1024]{1,0:T(8,128)(2,1)S(1)} %bitcast.167, bf16[1024,1024]{1,0:T(8,128)(2,1)S(1)} %bitcast.226), kind=kOutput, calls=%fused_computation.132 | convolution fusion | flops 1087372288 | bytes 6299648 | tf_op jit(solution)/shard_map/dot_general | solution.py:45
  97.5 3.0 %convolution_convert_fusion.1 = bf16[1024,1024]{1,0:T(8,128)(2,1)} fusion(bf16[512,1024]{1,0:T(8,128)(2,1)S(1)} %bitcast.168, f32[512,1024]{1,0:T(8,128)S(1)} %fusion.73, f32[1024]{0:T(1024)S(1)} %bitcast.211), kind=kOutput, calls=%fused_computation.31 | convolution fusion | flops 1080033280 | bytes 5246976 | tf_op jit(solution)/shard_map/dot_general | solution.py:45
  100.5 2.3 convolution_convert_fusion.5
  102.8 1.3 convolution_convert_fusion
  104.1 1.5 copy.87
  105.6 15.8 %shard_map.246 = (bf16[4,128,1024]{2,1,0:T(8,128)(2,1)}, bf16[4,128,1024]{2,1,0:T(8,128)(2,1)}, bf16[4,4,32,1024]{3,2,1,0:T(8,128)(2,1)}) custom-call(bf16[4,128,1024]{2,1,0:T(8,128)(2,1)} %bitcast.177, bf16[2,4,128,1024]{3,2,1,0:T(8,128)(2,1)} %bitcast.173, bf16[2,4,4,32,1024]{4,3,2,1,0:T(8,128)(2,1)} %bitcast.170), custom_call_target="tpu_custom_call" | custom-call | tf_op jit(solution)/shard_map/pallas_call | solution.py:415
  121.4 2.8 fusion.14.refs_1_
  124.2 0.5 multiply_reduce_fusion
  124.7 1.1 copy-done.18
  126.1 1.4 fusion.15.refs_2_
  127.8 0.4 copy-done.25
  128.1 1.1 convolution_convert_fusion.7
  129.4 0.9 copy.58
  130.4 0.8 convolution_convert_fusion.2
  131.2 1.5 copy.86
  132.7 31.7 %shard_map.247 = (bf16[4,128,256]{2,1,0:T(8,128)(2,1)}, bf16[4,128,1024]{2,1,0:T(8,128)(2,1)}, bf16[4,128,1024]{2,1,0:T(8,128)(2,1)}, bf16[4,128,1024]{2,1,0:T(8,128)(2,1)}) custom-call(bf16[4,128,256]{2,1,0:T(8,128)(2,1)} %bitcast.178, bf16[4,128,1024]{2,1,0:T(8,128)(2,1)} %bitcast.175, bf16[4,128,1024]{2,1,0:T(8,128)(2,1)} %fusion.15.refs_2_, ...), custom_call_target="tpu_custom_call" | custom-call | tf_op jit(solution)/shard_map/pallas_call | solution.py:415
  164.4 2.5 add_bitcast_fusion
  166.8 2.8 fusion.13.refs_2_
  169.6 1.2 fusion.37
  171.3 0.4 copy-done.31
  171.9 4.5 %fusion.2 = f32[4,512,512]{1,2,0:T(8,128)} fusion(pred[512,512]{0,1:T(8,128)(4,1)S(1)} %copy-done.37, bf16[4,512,64]{1,2,0:T(8,128)(2,1)S(1)} %bitcast.197, bf16[4,512,64]{1,2,0:T(8,128)(2,1)S(1)} %bitcast.195), kind=kOutput, calls=%fused_computation.3 | convolution fusion | flops 273680896 | bytes 4980736 | tf_op jit(solution)/shard_map/reduce_sum | solution.py:1112
  176.4 3.1 %fusion.16 = f32[4,512,64]{1,2,0:T(8,128)S(1)} fusion(f32[4,512,512]{1,2,0:T(8,128)} %fusion.2, bf16[512,4,64]{0,2,1:T(8,128)(2,1)S(1)} %reshape_reshape.3), kind=kOutput, calls=%fused_computation.24 | convolution fusion | flops 135266304 | bytes 4980736 | tf_op jit(solution)/shard_map/hqk,hqd->hkd/dot_general | solution.py:1173
  179.5 0.4 copy-done.10
  179.8 0.8 multiply_convert_fusion
  180.6 0.8 convolution_multiply_fusion.1
  181.6 0.5 convolution_multiply_fusion
  182.0 0.9 copy-done.43
  183.0 2.0 convolution_convert_fusion.4
  185.2 1.1 convolution_convert_fusion.3
  186.3 1.3 copy.88
  187.7 48.1 %shard_map.248 = (bf16[4,128,1024]{2,1,0:T(8,128)(2,1)}, bf16[4,4,32,1024]{3,2,1,0:T(8,128)(2,1)}, bf16[4,128,1024]{2,1,0:T(8,128)(2,1)}, bf16[4,128,768]{2,1,0:T(8,128)(2,1)}) custom-call(bf16[4,128,1024]{2,1,0:T(8,128)(2,1)} %bitcast.176, bf16[4,4,32,1024]{3,2,1,0:T(8,128)(2,1)} %fusion.14.refs_1_, bf16[4,128,1024]{2,1,0:T(8,128)(2,1)} %fusion.13.refs_2_, ...), custom_call_target="tpu_custom_call" | custom-call | tf_op jit(solution)/shard_map/pallas_call | solution.py:415
  235.9 2.4 add_convert_fusion
  238.3 1.1 fusion.47.refs_1_
  239.4 0.5 fusion.60
  240.0 1.1 fusion.21.refs_0_
  241.5 1.1 convert_reduce_fusion.1
  243.0 0.6 reshape.440.refs_3_
  243.6 17.3 %shard_map.249 = (bf16[4,128,768]{2,1,0:T(8,128)(2,1)}, bf16[4,32,1024]{2,1,0:T(8,128)(2,1)}, bf16[4,32,1024]{2,1,0:T(8,128)(2,1)}, f32[32,3,128]{2,1,0:T(4,128)}) custom-call(bf16[4,128,768]{2,1,0:T(8,128)(2,1)} %fusion.21.refs_0_, bf16[4,32,1024]{2,1,0:T(8,128)(2,1)} %fusion.47.refs_1_, bf16[4,32,1024]{2,1,0:T(8,128)(2,1)} %bitcast.179, ...), custom_call_target="tpu_custom_call" | custom-call | tf_op jit(solution)/shard_map/pallas_call | solution.py:415
  260.9 1.7 add_bitcast_fusion.1
  262.6 2.1 add_convert_fusion.2
  264.9 0.6 slice.321
  265.4 0.5 slice_bitcast_fusion
  266.0 0.6 fusion.72
  266.5 9.1 %shard_map.250 = bf16[4,32,768]{2,1,0:T(8,128)(2,1)} custom-call(bf16[4,32,768]{2,1,0:T(8,128)(2,1)} %bitcast.191), custom_call_target="tpu_custom_call" | custom-call | tf_op jit(solution)/shard_map/pallas_call | solution.py:415
  275.7 1.1 select_convert_fusion
  277.3 0.9 reshape.467
  278.4 0.8 copy.79
  (119 shorter events, 4.5 us)
Async XLA Ops:
  3.5 0.9 copy-start
  4.5 0.9 copy-start.2
  5.4 0.9 copy-start.4
  6.4 0.9 copy-start.5
  7.3 0.9 copy-start.6
  8.3 0.8 copy-start.7
  82.3 1.0 copy-start.8
  89.1 3.0 %copy-start.42 = (bf16[2,4,128,1024]{3,2,1,0:T(8,128)(2,1)S(1)}, bf16[2,4,128,1024]{3,2,1,0:T(8,128)(2,1)}, u32[]{:S(2)}) copy-start(bf16[2,4,128,1024]{3,2,1,0:T(8,128)(2,1)} %get-tuple-element.46) | copy-start | bytes 6291460
  92.1 2.5 copy-start.9
  97.5 3.0 %copy-start.41 = (bf16[4,2,4,32,1024]{4,3,2,1,0:T(8,128)(2,1)S(1)}, bf16[4,2,4,32,1024]{4,3,2,1,0:T(8,128)(2,1)}, u32[]{:S(2)}) copy-start(bf16[4,2,4,32,1024]{4,3,2,1,0:T(8,128)(2,1)} %get-tuple-element.44) | copy-start | bytes 6291460
  105.6 15.8 %copy-start.12 = (bf16[4,2,4,32,1024]{4,3,0,2,1:T(8,128)(2,1)S(1)}, bf16[4,2,4,32,1024]{4,3,0,2,1:T(8,128)(2,1)}, u32[]{:S(2)}) copy-start(bf16[4,2,4,32,1024]{4,3,0,2,1:T(8,128)(2,1)} %copy.87) | copy-start | bytes 6291460
  121.4 2.8 %copy-start.21 = (bf16[512,1024]{1,0:T(8,128)(2,1)S(1)}, bf16[512,1024]{1,0:T(8,128)(2,1)}, u32[]{:S(2)}) copy-start(bf16[512,1024]{1,0:T(8,128)(2,1)} %convolution_convert_fusion.5) | copy-start | bytes 3145732
  121.4 2.8 %copy-start.30 = (bf16[4,128,1024]{2,1,0:T(8,128)(2,1)S(1)}, bf16[4,128,1024]{2,1,0:T(8,128)(2,1)}, u32[]{:S(2)}) copy-start(bf16[4,128,1024]{2,1,0:T(8,128)(2,1)} %get-tuple-element.48) | copy-start | bytes 3145732
  124.2 1.6 copy-start.18
  124.2 1.9 copy-start.27
  126.1 1.7 copy-start.3
  126.1 2.1 copy-start.25
  132.7 31.7 %copy-start.14 = (bf16[4,128,1024]{2,1,0:T(8,128)(2,1)S(1)}, bf16[4,128,1024]{2,1,0:T(8,128)(2,1)}, u32[]{:S(2)}) copy-start(bf16[4,128,1024]{2,1,0:T(8,128)(2,1)} %fusion.15.refs_2_) | copy-start | bytes 3145732
  164.4 2.5 copy-start.11
  166.8 2.8 copy-start.19
  166.8 2.8 copy-start.28
  169.6 1.2 copy-start.22
  169.6 1.2 copy-start.39
  170.8 1.0 copy-start.31
  170.8 1.0 copy-start.33
  170.8 1.1 copy-start.37
  176.4 3.4 %copy-start.10 = (f32[4,512,512]{1,2,0:T(8,128)S(1)}, f32[4,512,512]{1,2,0:T(8,128)}, u32[]{:S(2)}) copy-start(f32[4,512,512]{1,2,0:T(8,128)} %fusion.2) | copy-start | bytes 12582916
  176.4 3.5 %copy-start.34 = (bf16[512,256]{0,1:T(8,128)(2,1)S(1)}, bf16[512,256]{0,1:T(8,128)(2,1)}, u32[]{:S(2)}) copy-start(bf16[512,256]{0,1:T(8,128)(2,1)} %copy.63) | copy-start | bytes 786436
  180.6 1.0 copy-start.32
  181.6 1.4 copy-start.43
  183.0 2.2 copy-start.44
  187.7 48.1 %copy-start.16 = (bf16[4,128,1024]{2,1,0:T(8,128)(2,1)S(1)}, bf16[4,128,1024]{2,1,0:T(8,128)(2,1)}, u32[]{:S(2)}) copy-start(bf16[4,128,1024]{2,1,0:T(8,128)(2,1)} %fusion.13.refs_2_) | copy-start | bytes 3145732
  235.8 2.5 copy-start.15
  235.8 2.5 copy-start.29
  235.8 3.5 %copy-start.1 = (bf16[128,1024]{1,0:T(8,128)(2,1)S(1)}, bf16[128,1024]{1,0:T(8,128)(2,1)}, u32[]{:S(2)}) copy-start(bf16[128,1024]{1,0:T(8,128)(2,1)} %refs_0_.1) | copy-start | bytes 786436
  235.9 3.5 %copy-start.20 = (bf16[512,1024]{1,0:T(8,128)(2,1)S(1)}, bf16[512,1024]{1,0:T(8,128)(2,1)}, u32[]{:S(2)}) copy-start(bf16[512,1024]{1,0:T(8,128)(2,1)} %convolution_convert_fusion.4) | copy-start | bytes 3145732
  235.9 3.5 %copy-start.26 = (bf16[4,128,1024]{2,1,0:T(8,128)(2,1)S(1)}, bf16[4,128,1024]{2,1,0:T(8,128)(2,1)}, u32[]{:S(2)}) copy-start(bf16[4,128,1024]{2,1,0:T(8,128)(2,1)} %get-tuple-element.61) | copy-start | bytes 3145732
  238.3 1.6 copy-start.13
  238.3 1.7 copy-start.35
  241.4 19.5 %copy-start.23 = (bf16[1,128,1024]{2,1,0:T(8,128)(2,1)S(1)}, bf16[1,128,1024]{2,1,0:T(8,128)(2,1)}, u32[]{:S(2)}) copy-start(bf16[1,128,1024]{2,1,0:T(8,128)(2,1)} %add_convert_fusion) | copy-start | bytes 786436
  241.5 21.2 %copy-start.17 = (bf16[4,128,768]{2,1,0:T(8,128)(2,1)S(1)}, bf16[4,128,768]{2,1,0:T(8,128)(2,1)}, u32[]{:S(2)}) copy-start(bf16[4,128,768]{2,1,0:T(8,128)(2,1)} %fusion.21.refs_0_) | copy-start | bytes 2359300
  243.6 21.1 %copy-start.36 = (f32[32,3,128]{2,1,0:T(4,128)S(1)}, f32[32,3,128]{2,1,0:T(4,128)}, u32[]{:S(2)}) copy-start(f32[32,3,128]{2,1,0:T(4,128)} %reshape.440.refs_3_) | copy-start | bytes 147460
  260.9 3.8 %copy-start.40 = (f32[32,3,128]{2,1,0:T(4,128)S(1)}, f32[32,3,128]{2,1,0:T(4,128)}, u32[]{:S(2)}) copy-start(f32[32,3,128]{2,1,0:T(4,128)} %get-tuple-element.65) | copy-start | bytes 147460
  264.7 13.5 %copy-start.24 = (bf16[4,32,1024]{2,1,0:T(8,128)(2,1)S(1)}, bf16[4,32,1024]{2,1,0:T(8,128)(2,1)}, u32[]{:S(2)}) copy-start(bf16[4,32,1024]{2,1,0:T(8,128)(2,1)} %fusion.47.refs_1_) | copy-start | bytes 786436
  264.7 13.5 %copy-start.38 = (bf16[4,32,1024]{2,1,0:T(8,128)(2,1)S(1)}, bf16[4,32,1024]{2,1,0:T(8,128)(2,1)}, u32[]{:S(2)}) copy-start(bf16[4,32,1024]{2,1,0:T(8,128)(2,1)} %get-tuple-element.68) | copy-start | bytes 786436

commit v3 on v2

--- a/solution.py
+++ b/solution.py
@@ -852,10 +852,365 @@
             *Spread.scratch(), *Spread.scratch(True), *Spread.scratch(True), *Spread.scratch(True),
             *Spread.scratch(),
         ],
+        compiler_params=pltpu.CompilerParams(collective_id=10, has_side_effects=True),
+    )(block_input, cotangent, qkv_weight, small, out_weight, fc_weight, proj_weight)
+
+
+def across(source, target, sems):
+    dp, s = place()
+    _, n = counts()
+    return [
+        remote(
+            source((s + k) % n), target(s), sems[0].at[k], sems[1].at[k], (dp, (s + k) % n)
+        )
+        for k in range(n - 1, 0, -1)
+    ]
+
+
+def around(source, target, sems):
+    dp, s = place()
+    dpc, _ = counts()
+    chip, core, nc = dp // 2, dp % 2, dpc // 2
+    return [
+        remote(
+            source((chip + k) % nc), target(chip), sems[0].at[k], sems[1].at[k],
+            ((chip + k) % nc * 2 + core, s),
+        )
+        for k in range(1, nc)
+    ]
+
+
+def norm_back(values, gain, upstream):
+    centred, scale = unit_rows(values)
+    unit = centred * scale
+    inner = upstream * gain
+    along = jnp.mean(inner * unit, axis=-1, keepdims=True)
+    branch = scale * (inner - jnp.mean(inner, axis=-1, keepdims=True) - unit * along)
+    return branch, upstream * unit
+
+
+def column_sum(values):
+    return jnp.sum(values, axis=0, keepdims=True)
+
+
+def backward(x_own, nv_all, g_all, fc_cols, proj_rows, qkv_cols, out_full, xn_all, qkv_all, att_all, att_own, mid_own, par_all, fcb_all, lt_all):
+    dpc, n = counts()
+    nc, ranks = dpc // 2, dpc * n
+    tok, depth = x_own.shape
+    units, rows = fc_cols.shape[1], depth // ranks
+    wide, length, many = depth // n, n * tok, nc * tok
+    heads, own_units, strip = wide // HD, units // (2 * n), n * rows
+    half, full = jnp.bfloat16, jnp.float32
+    sources = (
+        nv_all, g_all, fc_cols, proj_rows, fcb_all, mid_own, par_all, out_full, att_own, qkv_all,
+        att_all, lt_all, qkv_cols, xn_all, x_own,
+    )
+    count = len(sources)
+    tile = 256
+    buffers = (
+        ((many, tile), full), ((many, tile), full), ((many, units), half), ((many, units), half),
+        ((many, depth), half), ((many, depth), half), ((many, depth), half), ((many, depth), half),
+        ((units, depth), half), ((units // 2, depth), half), ((units // 2, depth), half),
+        ((units // 2, depth), half), ((depth, units), half), ((nc * strip, units), half),
+        ((n * nc * rows, units), half), ((n * nc * rows, units), half), ((tok, depth), half),
+        ((length, wide), half), ((depth, depth), half), ((nc * strip, depth), half),
+        ((nc * strip, depth), half), ((nc * strip, depth), half), ((tok, depth), full),
+        ((length, wide), full), ((length, wide), full), ((length, 3 * wide), half),
+        ((length, depth), half), ((length, depth), half), ((depth, 3 * wide), half),
+        ((nc * strip, 3 * wide), half), ((nc * strip, 3 * wide), half),
+        ((nc * strip, 3 * wide), half),
+    )
+
+    def kernel(*refs):
+        refs = list(refs)
+
+        def take(amount):
+            head = refs[:amount]
+            del refs[:amount]
+            return head
+
+        sources_in = take(count)
+        output, stream_out, proj_out, fc_out, out_out, qkv_out, vec_out, qv_out, fb_out = take(9)
+        held = take(count)
+        nv, g, wf, wp, fcb, mid, par, wo, atto, qkv, att, lt, wq, xn, xo = held
+        (
+            pre_s, gh_s, hid, ph, b2, b2g, fp, fpg, dp_, dpr, dpp, dpg, df, dfr, dfp, dfg, gas, gat,
+            do, dor, dop, dog, gm, dk, dv, grad, b1, b1g, dq_, dqr, dqp, dqg,
+        ) = take(len(buffers))
+        load = take(1)[0]
+        s_b2, s_fp, s_dp, s_dpz, s_df, s_dfz, s_ga, s_do, s_dop, s_b1, s_dq, s_dqp = (
+            take(2) for _ in range(12)
+        )
+        dp, s = place()
+        chip, core = dp // 2, dp % 2
+        mine = pl.ds(pl.multiple_of(s * tok, tok), tok)
+
+        loads = [
+            pltpu.make_async_copy(a, b, load.at[i])
+            for i, (a, b) in enumerate(zip(sources_in, held))
+        ]
+        for copy in loads:
+            copy.start()
+        greet_near()
+        for copy in loads[:5]:
+            copy.wait()
+
+        def feed(u, carry):
+            cols = pl.ds(pl.multiple_of(u * tile, tile), tile)
+            pre_s[...] = matmul(nv[...], wf[:, cols])
+            gh_s[...] = contract(g[...], wp[cols, :], (1, 1))
+            bias = fcb[7:8, pl.ds(pl.multiple_of(chip * units + u * tile, tile), tile)]
+
+            def block(r, summed):
+                at = pl.ds(pl.multiple_of(r * tok, tok), tok)
+                act = pre_s[at] + bias
+                square = act * act
+                bent = jnp.tanh(GELU_COEF * (act + 0.044715 * act * square))
+                hid[at, cols] = halved(0.5 * act * (1.0 + bent))
+                slope = 0.5 * (1.0 + bent) + (0.5 * act) * (1.0 - bent * bent) * (
+                    GELU_COEF * (1.0 + 3.0 * 0.044715 * square)
+                )
+                grad_pre = gh_s[at] * slope
+                ph[at, cols] = halved(grad_pre)
+                return summed + column_sum(grad_pre)
+
+            fb_out[0:1, cols] = lax.fori_loop(0, nc, block, jnp.zeros((1, tile), full))
+            return carry
+
+        lax.fori_loop(0, units // tile, feed, 0)
+
+        def ring(values, weight, dims, target, got, sems):
+            def block(k, carry):
+                to = (chip + k) % nc
+                at = pl.ds(pl.multiple_of(to * tok, tok), tok)
+                target[at] = halved(contract(values[at], weight[...], dims))
+
+                @pl.when(k < nc)
+                def _():
+                    remote(
+                        part(target, to, tok), part(got, chip, tok), sems[0].at[k], sems[1].at[k],
+                        (to * 2 + core, s),
+                    ).start()
+
+                return carry
+
+            lax.fori_loop(1, nc + 1, block, 0)
+
+        def ring_waits(target, got, sems):
+            return around(lambda i: part(target, i, tok), lambda i: part(got, i, tok), sems)
+
+        def summed(own, got, at, size, amount):
+            value = widened(part(own, at, size)[...])
+            for k in range(1, amount):
+                value = value + widened(part(got, (at + k) % amount, size)[...])
+            return value
+
+        ring(ph, wf, (1, 1), b2, b2g, s_b2)
+
+        def outer(left, right, target, size):
+            def block(r, carry):
+                at = pl.ds(pl.multiple_of(r * tile, tile), tile)
+                target[at] = halved(contract(left[:, at], right[...], (0, 0)))
+                return carry
+
+            lax.fori_loop(0, size // tile, block, 0)
+
+        def halves(target, got, sems, size):
+            return [
+                remote(
+                    part(target, c * 2 + 1 - core, size), part(got, c, size), sems[0].at[c],
+                    sems[1].at[c], (other_core(dp), s),
+                )
+                for c in range(nc)
+            ]
+
+        outer(hid, g, dp_, units)
+        swap_dp = remote(
+            part(dp_, 1 - core, units // 2), dpr, s_dp[0].at[0], s_dp[1].at[0],
+            (other_core(dp), s),
+        )
+        swap_dp.start()
+        outer(nv, ph, df, depth)
+        swap_df = halves(df, dfr, s_df, strip)
+        for copy in swap_df:
+            copy.start()
+        swap_dp.wait()
+
+        def add_dp(i, carry):
+            at = pl.ds(pl.multiple_of(i * own_units, own_units), own_units)
+            dpp[at] = halved(
+                widened(part(dp_, core * n + i, own_units)[...]) + widened(dpr[at])
+            )
+            return carry
+
+        lax.fori_loop(0, n, add_dp, 0)
+        send_dp = across(
+            lambda i: part(dpp, i, own_units), lambda i: part(dpg, i, own_units), s_dpz
+        )
+        for copy in send_dp:
+            copy.start()
+        ring(hid, wp, (1, 0), fp, fpg, s_fp)
+        for copy in swap_df:
+            copy.wait()
+
+        def add_df(j, carry):
+            c, i = j // n, j % n
+            own = part(df, (c * 2 + core) * n + i, rows)[...]
+            part(dfp, i * nc + c, rows)[...] = halved(
+                widened(own) + widened(part(dfr, j, rows)[...])
+            )
+            return carry
+
+        lax.fori_loop(0, nc * n, add_df, 0)
+        for copy in loads[5:]:
+            copy.wait()
+        for copy in ring_waits(b2, b2g, s_b2):
+            copy.wait()
+        grad_out = widened(part(g, chip, tok)[...])
+        upstream = summed(b2, b2g, chip, tok, nc)
+        branch, gains = norm_back(mid[...], par[3:4], upstream)
+        grad_middle = grad_out + branch
+        gm[...] = grad_middle
+        middle_half = halved(grad_middle)
+        gas[...] = halved(contract(middle_half, wo[...], (1, 1)))
+        send_ga = across(lambda i: lanes(gas, i, wide), lambda i: part(gat, i, tok), s_ga)
+        for copy in send_ga:
+            copy.start()
+        vec_out[2:3] = column_sum(grad_middle)
+        vec_out[3:4] = column_sum(gains)
+        vec_out[4:5] = column_sum(upstream)
+        vec_out[5:6] = column_sum(grad_out)
+        gat[mine] = gas[:, pl.ds(pl.multiple_of(s * wide, wide), wide)]
+        b1[pl.ds(0, tok)] = middle_half
+        outer(atto, b1.at[pl.ds(0, tok)], do, depth)
+        swap_do = halves(do, dor, s_do, strip)
+        for copy in swap_do:
+            copy.start()
+        dk[...] = jnp.zeros_like(dk)
+        dv[...] = jnp.zeros_like(dv)
+        for copy in send_ga:
+            copy.wait()
+        send_df = across(
+            lambda i: part(dfp, i, nc * rows), lambda i: part(dfg, i, nc * rows), s_dfz
+        )
+        for copy in send_df:
+            copy.start()
+        for copy in swap_do:
+            copy.wait()
+
+        def add_halves(own, got, target):
+            def block(c, carry):
+                part(target, c, strip)[...] = halved(
+                    widened(part(own, c * 2 + core, strip)[...])
+                    + widened(part(got, c, strip)[...])
+                )
+                return carry
+
+            lax.fori_loop(0, nc, block, 0)
+
+        add_halves(do, dor, dop)
+        send_do = around(lambda i: part(dop, i, strip), lambda i: part(dog, i, strip), s_dop)
+        for copy in send_do:
+            copy.start()
+        scale = HD ** (-0.5)
+        sums = jnp.zeros((1, 3 * wide), full)
+        for i in range(n - 1, -1, -1):
+            seen = (i + 1) * tok
+            here, past = pl.ds(i * tok, tok), pl.ds(0, seen)
+            queries_back = []
+            for p in range(wide // 128):
+                group = pl.ds(p * 128, 128)
+                q2 = qkv[here, group]
+                k2 = qkv[past, pl.ds(wide + p * 128, 128)]
+                v2 = qkv[past, pl.ds(2 * wide + p * 128, 128)]
+                ga2, att2 = gat[here, group], widened(att[here, group])
+                d_query = jnp.zeros((tok, 128), full)
+                d_key = jnp.zeros((seen, 128), full)
+                d_value = jnp.zeros((seen, 128), full)
+                for h in range(2):
+                    mask = mask_of(h, q2.shape)
+                    qm = jnp.where(mask, q2, jnp.zeros_like(q2))
+                    gam = jnp.where(mask, ga2, jnp.zeros_like(ga2))
+                    km = jnp.where(mask_of(h, k2.shape), k2, jnp.zeros_like(k2))
+                    probs, _ = softmax_block(qm, k2, lt[2 * p + h, here], i * tok)
+                    delta = jnp.sum(widened(gam) * att2, axis=-1, keepdims=True)
+                    grad_scores = halved(probs * (contract(gam, v2, (1, 1)) - delta))
+                    d_query = d_query + matmul(grad_scores, km)
+                    d_key = d_key + contract(grad_scores, qm, (0, 0))
+                    d_value = d_value + contract(halved(probs), gam, (0, 0))
+                dk[past, group] = dk[past, group] + d_key
+                dv[past, group] = dv[past, group] + d_value
+                queries_back.append(d_query * scale)
+            packed = jnp.concatenate(queries_back + [dk[here] * scale, dv[here]], axis=1)
+            sums = sums + column_sum(packed)
+            packed = halved(packed)
+            grad[here] = packed
+            b1[here] = halved(contract(packed, wq[...], (1, 1)))
+
+            @pl.when(i != s)
+            def _():
+                k = (i - s + n) % n
+                remote(
+                    part(b1, i, tok), part(b1g, s, tok), s_b1[0].at[k], s_b1[1].at[k], (dp, i)
+                ).start()
+
+        qv_out[0:1] = sums
+        outer(xn, grad, dq_, depth)
+        swap_dq = halves(dq_, dqr, s_dq, strip)
+        for copy in swap_dq:
+            copy.start()
+        for copy in ring_waits(fp, fpg, s_fp):
+            copy.wait()
+        output[...] = mid[...] + summed(fp, fpg, chip, tok, nc) + par[5:6]
+        for copy in swap_dq:
+            copy.wait()
+        add_halves(dq_, dqr, dqp)
+        send_dq = around(lambda i: part(dqp, i, strip), lambda i: part(dqg, i, strip), s_dqp)
+        for copy in send_dq:
+            copy.start()
+        for copy in send_dp:
+            copy.wait()
+        proj_out[...] = summed(dpp, dpg, s, own_units, n)
+        for copy in send_do:
+            copy.wait()
+        out_out[...] = halved(summed(dop, dog, chip, strip, nc))
+        for copy in send_dq:
+            copy.wait()
+        qkv_out[...] = halved(summed(dqp, dqg, chip, strip, nc))
+        for copy in across(lambda i: part(b1, i, tok), lambda i: part(b1g, i, tok), s_b1):
+            copy.wait()
+        upstream = summed(b1, b1g, s, tok, n)
+        branch, gains = norm_back(widened(xo[...]), par[0:1], upstream)
+        stream_out[...] = gm[...] + branch
+        vec_out[0:1] = column_sum(gains)
+        vec_out[1:2] = column_sum(upstream)
+        for copy in send_df:
+            copy.wait()
+        fc_out[...] = halved(summed(dfp, dfg, s, nc * rows, n))
+
+    def shape(kind, *dims):
+        return jax.ShapeDtypeStruct(dims, kind)
+
+    return pl.pallas_call(
+        kernel,
+        out_shape=[
+            shape(full, tok, depth), shape(full, tok, depth), shape(full, own_units, depth),
+            shape(half, nc * rows, units), shape(half, strip, depth), shape(half, strip, 3 * wide),
+            shape(full, 8, depth), shape(full, 8, 3 * wide), shape(full, 8, units),
+        ],
+        in_specs=[pl.BlockSpec(memory_space=pl.ANY)] * count,
+        out_specs=[pl.BlockSpec(memory_space=pltpu.VMEM)] * 9,
+        scratch_shapes=[pltpu.VMEM(a.shape, a.dtype) for a in sources]
+        + [pltpu.VMEM(dims, kind) for dims, kind in buffers]
+        + [
+            dma(count),
+            *[dma(nc)] * 4, *[dma(1)] * 2, *[dma(n)] * 2, *[dma(nc)] * 2, *[dma(n)] * 4,
+            *[dma(nc)] * 4, *[dma(n)] * 2, *[dma(nc)] * 4,
+        ],
         compiler_params=pltpu.CompilerParams(
-            collective_id=10, has_side_effects=True, vmem_limit_bytes=48 << 20
+            collective_id=11, has_side_effects=True, vmem_limit_bytes=67043328
         ),
-    )(block_input, cotangent, qkv_weight, small, out_weight, fc_weight, proj_weight)
+    )(*sources)
 
 
 def plain(
@@ -1086,118 +1441,22 @@
         small = small + row_of(parts[i], i)
     (
         normed_all, g_all, fc_all, proj_all, _, qkv_cols, out_full, xn_all, qkv, attended, attended_own,
-        middle, par, fcb, _,
+        middle, par, fcb, log_totals,
     ) = forward(block_input, cotangent, qkv_weight, small, out_weight, fc_weight, proj_weight)
-    grad_ff = g_all.reshape(nc * tok_rows, D)
-    fc_cols = fc_all.reshape(D, units)
-    proj_rows = proj_all.reshape(units, D)
-    gain_one, bias_one, out_bias_full, gain_two, bias_two, proj_bias_full = (par[i] for i in range(6))
-    fc_bias_cols = lax.dynamic_slice_in_dim(fcb[7], chip * units, units, 0)
-
-    def by_head(values):
-        return values.reshape(length, heads, HD).transpose(1, 0, 2)
-
-    def by_token(values):
-        return values.transpose(1, 0, 2).reshape(length, wide)
-
-    normed_one = xn_all
-    queries, keys, values = (by_head(qkv[:, i * wide : (i + 1) * wide]) for i in range(3))
-    attended_heads = by_head(attended)
-    position = jnp.arange(length, dtype=jnp.int32)
-    visible = position[None, :] <= position[:, None]
-    scores = (
-        jnp.einsum("hqd,hkd->hqk", queries, keys, preferred_element_type=jnp.float32) * score_scale
-    )
-    log_total = jnp.log(
-        jnp.sum(jnp.where(visible, jnp.exp(scores), 0.0), axis=-1, keepdims=True)
-    )
-    probs = jnp.where(visible, jnp.exp(scores - log_total), 0.0)
-    shares = halved(probs)
-    stream = widened(block_input)
-    normed_ff = normed_all.reshape(nc * tok_rows, D)
-    grad_out = widened(cotangent)
-    d_proj_bias = jnp.sum(grad_out, axis=0)
-    pre_act = matmul(normed_ff, fc_cols) + fc_bias_cols
-    hidden = halved(gelu_tanh(pre_act))
-    grad_hidden = matmul(grad_ff, proj_rows.T)
-    _, gelu_back = jax.vjp(gelu_tanh, pre_act)
-    grad_pre = gelu_back(grad_hidden)[0]
-    pre_half = halved(grad_pre)
-    back_two = halved(matmul(pre_half, fc_cols.T)).reshape(nc, tok_rows, D)
-    ff_part = halved(matmul(hidden, proj_rows)).reshape(nc, tok_rows, D)
-    d_proj = halved(matmul(hidden.T, grad_ff)).reshape(2, n, own_units, D)
-    d_fc = (
-        halved(matmul(normed_ff.T, pre_half))
-        .reshape(nc, 2, n, rows, units)
-        .transpose(1, 2, 0, 3, 4)
-    )
-    d_fc_bias = jnp.sum(grad_pre, axis=0)
-    back_two_got, d_proj_got, d_fc_got = run(
-        3, greet_near, Plane(back_two), Partner(d_proj), Partner(d_fc)
-    )
-
-    def pair(own, received):
-        kept = lax.dynamic_index_in_dim(own, core, 0, keepdims=False)
-        return halved(widened(kept) + widened(received))
-
-    _, norm_back_two = jax.vjp(layer_norm, middle, gain_two, bias_two)
-    mid_branch, d_ln2_gain, d_ln2_bias = norm_back_two(total(back_two, back_two_got, chip))
-    grad_middle = grad_out + mid_branch
-    d_out_bias = jnp.sum(grad_middle, axis=0)
-    middle_half = halved(grad_middle)
-    d_out = (
-        halved(matmul(attended_own.T, middle_half))
-        .reshape(nc, 2, n * rows, D)
-        .transpose(1, 0, 2, 3)
-    )
-    grad_attended = halved(matmul(middle_half, out_full.T))
-    grad_attended = grad_attended.reshape(tok_rows, n, wide).transpose(1, 0, 2)
-    d_proj, d_fc = pair(d_proj, d_proj_got), pair(d_fc, d_fc_got)
-    grad_att_got, ff_got, d_proj_parts, d_out_got = run(
-        4, greet_near, Exchange(grad_attended), Plane(ff_part), Exchange(d_proj), Partner(d_out)
-    )
-    proj_grad = total(d_proj, d_proj_parts, s)
-    output = middle + total(ff_part, ff_got, chip) + proj_bias_full
-    grad_att = by_head(fill(grad_attended, grad_att_got, s).reshape(length, wide))
-    row_delta = jnp.sum(widened(grad_att) * widened(attended_heads), axis=-1, keepdims=True)
-    grad_shares = jnp.einsum("hqd,hkd->hqk", grad_att, values, preferred_element_type=jnp.float32)
-    grad_scores = halved(probs * (grad_shares - row_delta))
-    grad_q = (
-        jnp.einsum("hqk,hkd->hqd", grad_scores, keys, preferred_element_type=jnp.float32)
-        * score_scale
-    )
-    grad_k = (
-        jnp.einsum("hqk,hqd->hkd", grad_scores, queries, preferred_element_type=jnp.float32)
-        * score_scale
-    )
-    grad_v = jnp.einsum("hqk,hqd->hkd", shares, grad_att, preferred_element_type=jnp.float32)
-    grad_qkv = jnp.concatenate([by_token(grad_q), by_token(grad_k), by_token(grad_v)], axis=1)
-    qkv_half = halved(grad_qkv)
-    back_one = halved(matmul(qkv_half, qkv_cols.T)).reshape(n, tok_rows, D)
-    d_qkv = (
-        halved(matmul(normed_one.T, qkv_half))
-        .reshape(nc, 2, n * rows, 3 * wide)
-        .transpose(1, 0, 2, 3)
-    )
-    sums = jnp.sum(grad_qkv, axis=0)
-    d_qv = jnp.stack([sums[:wide], sums[2 * wide :]])[:, None]
-    d_out = pair(d_out, d_out_got)
-    back_one_got, d_fc_parts, d_out_parts, d_qkv_got = run(
-        5, greet_near, Exchange(back_one), Exchange(d_fc), Plane(d_out), Partner(d_qkv)
-    )
-    d_qkv = pair(d_qkv, d_qkv_got)
-    fc_cut = halved(total(d_fc, d_fc_parts, s))
-    out_cut = halved(total(d_out, d_out_parts, chip)).reshape(n, rows, D)
-    _, norm_back_one = jax.vjp(layer_norm, stream, gain_one, bias_one)
-    stream_branch, d_ln1_gain, d_ln1_bias = norm_back_one(total(back_one, back_one_got, s))
-    grad_stream = grad_middle + stream_branch
+    output, grad_stream, proj_grad, fc_cut, out_cut, qkv_rows, vecs, qv_sums, fc_sums = backward(
+        block_input, normed_all.reshape(nc * tok_rows, D), g_all.reshape(nc * tok_rows, D),
+        fc_all.reshape(D, units), proj_all.reshape(units, D), qkv_cols, out_full, xn_all, qkv, attended,
+        attended_own, middle, par, fcb, log_totals,
+    )
+    fc_cut = fc_cut.reshape(nc, rows, units)
+    out_cut = out_cut.reshape(n, rows, D)
+    qkv_rows = qkv_rows.reshape(n, rows, 3 * wide)
+    d_qv = jnp.stack([qv_sums[0, :wide], qv_sums[0, 2 * wide :]])[:, None]
+    d_fc_bias = fc_sums[0]
     turn = jnp.arange(n, dtype=jnp.int32)[None, :, None] == s
     mine = jnp.arange(nc, dtype=jnp.int32)[:, None] == chip
     vectors = jnp.concatenate(
-        [
-            v.reshape(ranks, rows)
-            for v in (d_ln1_gain, d_ln1_bias, d_out_bias, d_ln2_gain, d_ln2_bias, d_proj_bias)
-        ]
+        [vecs[:6].reshape(6, ranks, rows).transpose(1, 0, 2).reshape(ranks, 6 * rows)]
         + [
             jnp.where(turn, d_qv, 0.0).reshape(ranks, -1),
             jnp.where(mine, d_fc_bias, 0.0).reshape(ranks, own_units),
@@ -1206,19 +1465,17 @@
     )
     used = vectors.shape[1]
     vectors = jnp.pad(vectors, ((0, 0), (0, -used % 128))).reshape(ranks, -1, 128)
-    d_qkv_parts, fc_got, d_out_last, vectors_got = run(
-        6, greet_all, Plane(d_qkv), Plane(fc_cut), Exchange(out_cut), Everyone(vectors)
+    qkv_got, fc_got, d_out_last, vectors_got = run(
+        6, greet_all, Exchange(qkv_rows), Plane(fc_cut), Exchange(out_cut), Everyone(vectors)
     )
     fc_grad = widened(fill(fc_cut, fc_got, chip)).transpose(1, 0, 2).reshape(rows, FF)
     out_grad = total(out_cut, d_out_last, s)
-    qkv_rows = halved(total(d_qkv, d_qkv_parts, chip)).reshape(n, rows, 3 * wide)
     vector = jnp.sum(fill(vectors, vectors_got, dp * n + s), axis=0).reshape(-1)
     firsts = [vector[i * rows : (i + 1) * rows] for i in range(6)]
     at = 6 * rows
     qv_grad = vector[at : at + qv_bias.shape[0]]
     at += qv_bias.shape[0]
     fc_bias_grad = vector[at : at + own_units]
-    (qkv_got,) = run(7, greet_seq, Exchange(qkv_rows))
     qkv_grad = (
         widened(fill(qkv_rows, qkv_got, s))
         .reshape(n, rows, 3, wide)
@@ -1232,9 +1489,9 @@
 
 
 def local(*arrays):
-    _, n = counts()
+    dpc, n = counts()
     fits = (D // n) % 128 == 0 and arrays[4].shape[0] % 16 == 0 and arrays[0].shape[0] % 128 == 0
-    return fused(*arrays) if fits else plain(*arrays)
+    return fused(*arrays) if fits and FF // (dpc // 2) % 256 == 0 else plain(*arrays)
 
 
 def solution(mesh):

time: 280 us -> 200 us (0.71)
  matrix products: 29.3 us -> 0 us
  other arithmetic: 26.5 us -> 3.76 us
  local copies, waits for them, and re-layouts: 27 us -> 9.78 us
  Pallas kernels: 195 us -> 186 us
    pallas_call x5 -> x1, Pallas kernels: 122 us -> 17.9 us  [run(): pl.pallas_call(kernel, out_shape=[jax.ShapeDtypeStruct(o.shape, o.dtype)...]
    pallas_call x0 -> x1, Pallas kernels: none -> 94.4 us  [backward(): pl.pallas_call(kernel, out_shape=[shape(full, tok, depth), shape(full, to...]
    dot_general x14 -> x0, matrix products: 24.9 us -> none  [the longest x10 19.8 us: matmul(): return jnp.dot(left, right, preferred_element_type=jnp.float32)]
    convert_element_type x7 -> x0, other arithmetic: 13.6 us -> none  [halved(): return values.astype(jnp.bfloat16)]
    unnamed x90 -> x21, local copies, waits for them, and re-layouts: 10.7 us -> 2.42 us
    reshape x10 -> x3, local copies, waits for them, and re-layouts: 5.52 us -> 1 us  [fused(): vecs[:6].reshape(6, ranks, rows).transpose(1, 0, 2).reshape(ranks, 6 * rows)]
    reduce_sum x1 -> x0, matrix products: 4.46 us -> none  [fused(): jnp.sum(jnp.where(visible, jnp.exp(scores), 0.0), axis=-1, keepdims=True)]
    reduce_sum x10 -> x0, other arithmetic: 4.38 us -> none  [the longest x3 1.34 us: layer_norm(): return centred * lax.rsqrt(spread + EPS) * norm_gain + offset]
where the time goes in v3:
time: 200 us
  Pallas kernels  186 us (93%)
  local copies, waits for them, and re-layouts  9.78 us (5%)
  other arithmetic  3.76 us (2%)
    pallas_call x1, Pallas kernels, backward(): pl.pallas_call(kernel, out_shape=[shape(full, tok, depth), shape(full, to...  94.4 us
    pallas_call x1, Pallas kernels, forward(): pl.pallas_call(kernel, out_shape=[shape(half, nc, tok, depth), shape(half...  73.4 us
    pallas_call x1, Pallas kernels, run(): pl.pallas_call(kernel, out_shape=[jax.ShapeDtypeStruct(o.shape, o.dtype)...  17.9 us

profile of v3, /device:TPU:0, one launch (start us, length us, event | category | flops | bytes accessed | tf_op | source)
XLA Modules:
  0.0 200.0 jit_solution(8424581618976354333)
XLA Ops:
  0.6 1.4 pad_add_fusion.refs_3_
  2.0 73.4 %shard_map.245 = (bf16[4,128,1024]{2,1,0:T(8,128)(2,1)}, bf16[4,128,1024]{2,1,0:T(8,128)(2,1)}, bf16[4,2,4,32,1024]{4,3,2,1,0:T(8,128)(2,1)}, bf16[2,4,128,1024]...) custom-call(bf16[128,1024]{1,0:T(8,128)(2,1)} %refs_14_.1, ...), custom_call_target="tpu_custom_call" | custom-call | tf_op jit(solution)/shard_map/pallas_call | solution.py:830
  75.4 94.4 %shard_map.246 = (f32[128,1024]{1,0:T(8,128)}, f32[128,1024]{1,0:T(8,128)}, f32[128,1024]{1,0:T(8,128)}, bf16[128,1024]{1,0:T(8,128)(2,1)}, bf16[128,1024]{1,0:T...) custom-call(bf16[512,1024]{1,0:T(8,128)(2,1)} %bitcast.45, ...), custom_call_target="tpu_custom_call" | custom-call | tf_op jit(solution)/shard_map/pallas_call | solution.py:1194
  169.8 0.0 copy-start
  169.8 0.8 fusion.3
  170.6 0.1 broadcast_select_fusion
  170.6 0.1 select_n.57
  170.7 0.8 reshape.134
  171.6 0.0 copy-start.1
  171.6 0.1 copy.37
  171.7 0.1 reshape.135
  171.7 0.8 slice.70
  172.5 0.1 broadcast_in_dim.107
  172.6 0.1 broadcast_in_dim.108
  172.7 0.1 bitcast_select_fusion
  172.8 0.1 pad_maximum_fusion
  172.8 0.7 reshape.136.refs_3_
  173.5 17.9 %shard_map.247 = (bf16[4,32,768]{2,1,0:T(8,128)(2,1)}, bf16[4,32,1024]{2,1,0:T(8,128)(2,1)}, bf16[4,32,1024]{2,1,0:T(8,128)(2,1)}, f32[32,3,128]{2,1,0:T(4,128)}) custom-call(bf16[4,32,768]{2,1,0:T(8,128)(2,1)} %bitcast.50, bf16[4,32,1024]{2,1,0:T(8,128)(2,1)} %bitcast.48, bf16[4,32,1024]{2,1,0:T(8,128)(2,1)} %bitcast.47, f32[32,3,128]{2,1,0:T(4,128)} %reshape.136.refs_3_), custom_call_target="tpu_custom_call" | custom-call | tf_op jit(solution)/shard_map/pallas_call | solution.py:415
  191.4 0.0 copy-start.6
  191.5 0.0 copy-start.7
  191.5 1.2 convert_bitcast_fusion
  192.7 0.8 copy.35
  193.5 0.0 copy-start.2
  193.5 0.0 copy-start.8
  193.5 0.0 copy-done
  193.5 0.0 copy-done.6
  193.5 0.0 copy-start.5
  193.5 0.7 fusion
  194.2 0.0 copy-done.1
  194.2 0.0 copy-done.7
  194.2 0.1 select_convert_fusion
  194.3 0.0 copy-start.4
  194.4 0.2 reshape.157
  194.6 0.0 copy-start.3
  194.6 0.3 copy.33
  194.8 0.9 reshape.147
  195.8 0.0 copy-done.2
  195.8 0.0 copy-done.8
  195.8 0.1 select_reduce_fusion
  195.9 0.6 fusion.4
  196.5 0.6 slice.73
  197.1 0.5 slice_bitcast_fusion
  197.6 0.0 copy-done.5
  197.6 0.8 copy.41
  198.4 0.0 copy-done.4
  198.4 0.8 copy.42
  199.2 0.0 copy-done.3
  199.2 0.8 copy.43
  (4 shorter events, 0.0 us)
Async XLA Ops:
  169.8 23.7 %copy-start = (bf16[128,1024]{1,0:T(8,128)(2,1)S(1)}, bf16[128,1024]{1,0:T(8,128)(2,1)}, u32[]{:S(2)}) copy-start(bf16[128,1024]{1,0:T(8,128)(2,1)} %get-tuple-element.62) | copy-start | bytes 786436
  171.6 22.7 %copy-start.1 = (bf16[128,768]{1,0:T(8,128)(2,1)S(1)}, bf16[128,768]{1,0:T(8,128)(2,1)}, u32[]{:S(2)}) copy-start(bf16[128,768]{1,0:T(8,128)(2,1)} %get-tuple-element.60) | copy-start | bytes 589828
  191.4 2.1 %copy-start.6 = (bf16[4,32,1024]{2,1,0:T(8,128)(2,1)S(1)}, bf16[4,32,1024]{2,1,0:T(8,128)(2,1)}, u32[]{:S(2)}) copy-start(bf16[4,32,1024]{2,1,0:T(8,128)(2,1)} %get-tuple-element.65) | copy-start | bytes 786436
  191.5 2.8 %copy-start.7 = (bf16[4,32,768]{2,1,0:T(8,128)(2,1)S(1)}, bf16[4,32,768]{2,1,0:T(8,128)(2,1)}, u32[]{:S(2)}) copy-start(bf16[4,32,768]{2,1,0:T(8,128)(2,1)} %get-tuple-element.64) | copy-start | bytes 589828
  193.5 2.3 %copy-start.2 = (f32[32,3,128]{2,1,0:T(4,128)S(1)}, f32[32,3,128]{2,1,0:T(4,128)}, u32[]{:S(2)}) copy-start(f32[32,3,128]{2,1,0:T(4,128)} %reshape.136.refs_3_) | copy-start | bytes 147460
  193.5 2.3 %copy-start.8 = (f32[32,3,128]{2,1,0:T(4,128)S(1)}, f32[32,3,128]{2,1,0:T(4,128)}, u32[]{:S(2)}) copy-start(f32[32,3,128]{2,1,0:T(4,128)} %get-tuple-element.63) | copy-start | bytes 147460
  193.5 4.1 %copy-start.5 = (f32[128,1024]{1,0:T(8,128)S(1)}, f32[128,1024]{1,0:T(8,128)}, u32[]{:S(2)}) copy-start(f32[128,1024]{1,0:T(8,128)} %get-tuple-element.90) | copy-start | bytes 1572868
  194.3 4.1 %copy-start.4 = (f32[128,1024]{1,0:T(8,128)S(1)}, f32[128,1024]{1,0:T(8,128)}, u32[]{:S(2)}) copy-start(f32[128,1024]{1,0:T(8,128)} %get-tuple-element.91) | copy-start | bytes 1572868
  194.6 4.6 %copy-start.3 = (f32[128,1024]{1,0:T(8,128)S(1)}, f32[128,1024]{1,0:T(8,128)}, u32[]{:S(2)}) copy-start(f32[128,1024]{1,0:T(8,128)} %get-tuple-element.102) | copy-start | bytes 1572868

commit v4 on v3

--- a/solution.py
+++ b/solution.py
@@ -796,6 +796,9 @@
                 part(att, s, tok), lanes(atto, back, wide), att_send.at[k], att_recv.at[k],
                 (dp, back),
             ).wait_recv()
+        for k in range(2, min(n, 3)):
+            fc.step(k)
+            proj.step(k)
         middle = widened(xv[pl.ds(pl.multiple_of(s * tok, tok), tok)]) + matmul(
             atto[...], wo[...]
         ) + par[2:3]
@@ -807,7 +810,7 @@
         keep_n.start()
         for copy in saves[8:]:
             copy.start()
-        for k in range(2, n):
+        for k in range(3, n):
             fc.step(k)
             proj.step(k)
         grads.step()

time: 200 us -> 200 us (level)
  no operation moved by 1% of the time
where the time goes in v4:
time: 200 us
  Pallas kernels  186 us (93%)
  local copies, waits for them, and re-layouts  9.78 us (5%)
  other arithmetic  3.76 us (2%)
    pallas_call x1, Pallas kernels, backward(): pl.pallas_call(kernel, out_shape=[shape(full, tok, depth), shape(full, to...  94.4 us
    pallas_call x1, Pallas kernels, forward(): pl.pallas_call(kernel, out_shape=[shape(half, nc, tok, depth), shape(half...  73.4 us
    pallas_call x1, Pallas kernels, run(): pl.pallas_call(kernel, out_shape=[jax.ShapeDtypeStruct(o.shape, o.dtype)...  17.9 us

profile of v4, /device:TPU:0, one launch (start us, length us, event | category | flops | bytes accessed | tf_op | source)
XLA Modules:
  0.0 200.0 jit_solution(17912977279973949892)
XLA Ops:
  0.6 1.4 pad_add_fusion.refs_3_
  2.0 73.4 %shard_map.245 = (bf16[4,128,1024]{2,1,0:T(8,128)(2,1)}, bf16[4,128,1024]{2,1,0:T(8,128)(2,1)}, bf16[4,2,4,32,1024]{4,3,2,1,0:T(8,128)(2,1)}, bf16[2,4,128,1024]...) custom-call(bf16[128,1024]{1,0:T(8,128)(2,1)} %refs_14_.1, ...), custom_call_target="tpu_custom_call" | custom-call | tf_op jit(solution)/shard_map/pallas_call | solution.py:833
  75.4 94.4 %shard_map.246 = (f32[128,1024]{1,0:T(8,128)}, f32[128,1024]{1,0:T(8,128)}, f32[128,1024]{1,0:T(8,128)}, bf16[128,1024]{1,0:T(8,128)(2,1)}, bf16[128,1024]{1,0:T...) custom-call(bf16[512,1024]{1,0:T(8,128)(2,1)} %bitcast.45, ...), custom_call_target="tpu_custom_call" | custom-call | tf_op jit(solution)/shard_map/pallas_call | solution.py:1197
  169.8 0.0 copy-start
  169.8 0.8 fusion.3
  170.6 0.1 broadcast_select_fusion
  170.6 0.1 select_n.57
  170.7 0.8 reshape.134
  171.6 0.0 copy-start.1
  171.6 0.1 copy.37
  171.7 0.1 reshape.135
  171.7 0.8 slice.70
  172.5 0.1 broadcast_in_dim.107
  172.6 0.1 broadcast_in_dim.108
  172.7 0.1 bitcast_select_fusion
  172.8 0.1 pad_maximum_fusion
  172.8 0.7 reshape.136.refs_3_
  173.5 17.9 %shard_map.247 = (bf16[4,32,768]{2,1,0:T(8,128)(2,1)}, bf16[4,32,1024]{2,1,0:T(8,128)(2,1)}, bf16[4,32,1024]{2,1,0:T(8,128)(2,1)}, f32[32,3,128]{2,1,0:T(4,128)}) custom-call(bf16[4,32,768]{2,1,0:T(8,128)(2,1)} %bitcast.50, bf16[4,32,1024]{2,1,0:T(8,128)(2,1)} %bitcast.48, bf16[4,32,1024]{2,1,0:T(8,128)(2,1)} %bitcast.47, f32[32,3,128]{2,1,0:T(4,128)} %reshape.136.refs_3_), custom_call_target="tpu_custom_call" | custom-call | tf_op jit(solution)/shard_map/pallas_call | solution.py:415
  191.4 0.0 copy-start.6
  191.5 0.0 copy-start.7
  191.5 1.2 convert_bitcast_fusion
  192.7 0.8 copy.35
  193.5 0.0 copy-start.2
  193.5 0.0 copy-start.8
  193.5 0.0 copy-done
  193.5 0.0 copy-done.6
  193.5 0.0 copy-start.5
  193.5 0.7 fusion
  194.2 0.0 copy-done.1
  194.2 0.0 copy-done.7
  194.2 0.1 select_convert_fusion
  194.3 0.0 copy-start.4
  194.4 0.2 reshape.157
  194.6 0.0 copy-start.3
  194.6 0.3 copy.33
  194.8 0.9 reshape.147
  195.8 0.0 copy-done.2
  195.8 0.0 copy-done.8
  195.8 0.1 select_reduce_fusion
  195.9 0.6 fusion.4
  196.5 0.6 slice.73
  197.1 0.5 slice_bitcast_fusion
  197.6 0.0 copy-done.5
  197.6 0.8 copy.41
  198.4 0.0 copy-done.4
  198.4 0.8 copy.42
  199.2 0.0 copy-done.3
  199.2 0.8 copy.43
  (4 shorter events, 0.0 us)
Async XLA Ops:
  169.8 23.7 %copy-start = (bf16[128,1024]{1,0:T(8,128)(2,1)S(1)}, bf16[128,1024]{1,0:T(8,128)(2,1)}, u32[]{:S(2)}) copy-start(bf16[128,1024]{1,0:T(8,128)(2,1)} %get-tuple-element.62) | copy-start | bytes 786436
  171.6 22.7 %copy-start.1 = (bf16[128,768]{1,0:T(8,128)(2,1)S(1)}, bf16[128,768]{1,0:T(8,128)(2,1)}, u32[]{:S(2)}) copy-start(bf16[128,768]{1,0:T(8,128)(2,1)} %get-tuple-element.60) | copy-start | bytes 589828
  191.4 2.1 %copy-start.6 = (bf16[4,32,1024]{2,1,0:T(8,128)(2,1)S(1)}, bf16[4,32,1024]{2,1,0:T(8,128)(2,1)}, u32[]{:S(2)}) copy-start(bf16[4,32,1024]{2,1,0:T(8,128)(2,1)} %get-tuple-element.65) | copy-start | bytes 786436
  191.5 2.8 %copy-start.7 = (bf16[4,32,768]{2,1,0:T(8,128)(2,1)S(1)}, bf16[4,32,768]{2,1,0:T(8,128)(2,1)}, u32[]{:S(2)}) copy-start(bf16[4,32,768]{2,1,0:T(8,128)(2,1)} %get-tuple-element.64) | copy-start | bytes 589828
  193.5 2.3 %copy-start.2 = (f32[32,3,128]{2,1,0:T(4,128)S(1)}, f32[32,3,128]{2,1,0:T(4,128)}, u32[]{:S(2)}) copy-start(f32[32,3,128]{2,1,0:T(4,128)} %reshape.136.refs_3_) | copy-start | bytes 147460
  193.5 2.3 %copy-start.8 = (f32[32,3,128]{2,1,0:T(4,128)S(1)}, f32[32,3,128]{2,1,0:T(4,128)}, u32[]{:S(2)}) copy-start(f32[32,3,128]{2,1,0:T(4,128)} %get-tuple-element.63) | copy-start | bytes 147460
  193.5 4.1 %copy-start.5 = (f32[128,1024]{1,0:T(8,128)S(1)}, f32[128,1024]{1,0:T(8,128)}, u32[]{:S(2)}) copy-start(f32[128,1024]{1,0:T(8,128)} %get-tuple-element.90) | copy-start | bytes 1572868
  194.3 4.1 %copy-start.4 = (f32[128,1024]{1,0:T(8,128)S(1)}, f32[128,1024]{1,0:T(8,128)}, u32[]{:S(2)}) copy-start(f32[128,1024]{1,0:T(8,128)} %get-tuple-element.91) | copy-start | bytes 1572868
  194.6 4.6 %copy-start.3 = (f32[128,1024]{1,0:T(8,128)S(1)}, f32[128,1024]{1,0:T(8,128)}, u32[]{:S(2)}) copy-start(f32[128,1024]{1,0:T(8,128)} %get-tuple-element.102) | copy-start | bytes 1572868
